TPU v7x, 256 devices: a whole 4x4x8 slice. The times are simulated.
256 devices in a mesh: lat: 16 (over x, y_lo, core), lon: 16 (over z, y_hi).
Axes of the slice: x: 4, y: 4 (y_hi: 2, y_lo: 2; y = y_hi * 2 + y_lo), z: 8, core: 2. Of those that a mesh axis runs over, the one named last changes fastest.
Arguments:
- tokens: bfloat16 [16, 32, 128, 1024], P('lat', 'lon'), may hold values from -80 to 80
- w_qkv: bfloat16 [1024, 3072], replicated, may hold values from -0.1875 to 0.1875
- w_out: bfloat16 [1024, 1024], replicated, may hold values from -0.1875 to 0.1875
- tele_ids: int32 [16, 32, 8], P('lat', 'lon'), may hold values from 0 to 31, as said below
Outputs:
- mixed: bfloat16 [16, 32, 128, 1024], P('lat', 'lon')
Inputs may be any that keep to these rules, and one draw needn't show every extreme that they name: `tele_ids`: the 16 entries of one device's query tiles name exactly 1 tile columns of each lon device, lon device o holding the tile columns o * 2 to o * 2 + 1.
All inputs are finite; a program needn't handle non-finite values.
Results may differ from a plain program's by a relative error of at most 0.013.
The roundings to bfloat16 on the way count: a program that leaves them out, or rounds other values in their place, can miss the bound.
Values may be sent and summed in bfloat16 or wider, within the bound.
A program may use at most 128 MiB of HBM per device.

v0:
```python
import jax
import jax.numpy as jnp
from jax import lax
from jax.sharding import PartitionSpec as P

H = 16
HD = 64
BLOCK = 128


def padded_2(array, sides, width, wrap):
    for axis, dim in sides:
        size, length = (lax.axis_size(axis), array.shape[dim])
        up = [(i, (i + 1) % size) for i in range(size if wrap else size - 1)]
        down = [(j, i) for i, j in up]
        last = lax.slice_in_dim(array, length - width, length, axis=dim)
        first = lax.slice_in_dim(array, 0, width, axis=dim)
        before = lax.ppermute(last, axis, up)
        after = lax.ppermute(first, axis, down)
        array = jnp.concatenate([before, array, after], axis=dim)
    return array


def attend(query, pairs, usable):
    tile_count = query.shape[0]
    key_count = pairs.shape[1]
    model_width = query.shape[2]
    group_width = 2 * HD

    def one_group(group_index):
        column_start = group_index * group_width
        queries = lax.dynamic_slice_in_dim(query, column_start, group_width, 2)
        queries = queries.reshape(tile_count, BLOCK, 2, HD)
        key_part = lax.dynamic_slice_in_dim(pairs, column_start, group_width, 2)
        key_part = key_part.reshape(tile_count, key_count, 2, HD)
        value_part = lax.dynamic_slice_in_dim(pairs, model_width + column_start, group_width, 2)
        value_part = value_part.reshape(tile_count, key_count, 2, HD)
        scores = jnp.einsum(
            "tqhd,tkhd->thqk", queries, key_part, preferred_element_type=jnp.float32
        ) * HD ** (-0.5)
        scores = jnp.where(usable[:, None, None, :], scores, -1e30)
        peak = jnp.max(scores, axis=-1, keepdims=True)
        expos = jnp.exp(scores - peak)
        weights = (expos / jnp.sum(expos, axis=-1, keepdims=True)).astype(jnp.bfloat16)
        summed = jnp.einsum(
            "thqk,tkhd->tqhd", weights, value_part, preferred_element_type=jnp.float32
        )
        return summed.astype(jnp.bfloat16).reshape(tile_count, BLOCK, group_width)

    outputs = lax.map(one_group, jnp.arange(H // 2, dtype=jnp.int32))
    return outputs.transpose(1, 2, 0, 3).reshape(tile_count, BLOCK, model_width)


def take_row(panel_row, index_row):
    return jnp.take(panel_row, index_row, axis=0)


def fetch_far(material, tele_ids):
    tile_rows, tile_cols, block_len, carried = material.shape
    tele_count = tele_ids.shape[2]
    row_picks = tele_ids.reshape(tile_rows, tile_cols * tele_count)
    empty = jnp.zeros((tile_rows, tile_cols * tele_count, block_len, carried), material.dtype)
    piece = lax.all_gather(material, "lon", axis=1, tiled=True)
    count = piece.shape[1]
    inside = (row_picks >= 0) & (row_picks < count)
    grabbed = jax.vmap(take_row)(piece, jnp.clip(row_picks, 0, count - 1))
    far_tiles = jnp.where(inside[:, :, None, None], grabbed, empty)
    return far_tiles.reshape(tile_rows, tile_cols, tele_count, block_len, carried)


def on_device(tokens, w_qkv, w_out, tele_ids):
    tile_rows, tile_cols, block_len, model_width = tokens.shape
    tele_count = tele_ids.shape[2]
    pair_width = 2 * model_width
    flat_tokens = tokens.reshape(-1, model_width)
    projected = jnp.dot(flat_tokens, w_qkv, preferred_element_type=jnp.float32).astype(jnp.bfloat16)
    query = projected[:, :model_width]
    material = projected[:, model_width:].reshape(tile_rows, tile_cols, block_len, pair_width)
    query = query.reshape(tile_rows * tile_cols, block_len, model_width)
    beside_all = padded_2(material, (("lon", 1),), 1, True)
    padded = padded_2(beside_all, (("lat", 0),), 1, False)
    far_tiles = fetch_far(material, tele_ids)
    near_tiles = jnp.stack(
        [
            padded[lat_step : lat_step + tile_rows, lon_step : lon_step + tile_cols]
            for lat_step in range(3)
            for lon_step in range(3)
        ],
        axis=2,
    )
    pairs = jnp.concatenate([near_tiles, far_tiles], axis=2)
    pairs = pairs.reshape(tile_rows * tile_cols, (9 + tele_count) * block_len, pair_width)
    first_row = lax.axis_index("lat") * tile_rows
    total_rows = tile_rows * lax.axis_size("lat")
    lat_steps = jnp.array([0, 0, 0, 1, 1, 1, 2, 2, 2], dtype=jnp.int32)
    global_rows = (
        first_row + jnp.arange(tile_rows, dtype=jnp.int32)[:, None] + lat_steps[None, :] - 1
    )
    near_usable = (global_rows >= 0) & (global_rows < total_rows)
    usable = jnp.concatenate([near_usable, jnp.ones((tile_rows, tele_count), jnp.bool_)], axis=1)
    usable = jnp.repeat(usable, block_len, axis=1)
    usable = jnp.broadcast_to(usable[:, None, :], (tile_rows, tile_cols, usable.shape[1]))
    usable = usable.reshape(tile_rows * tile_cols, -1)
    attended = attend(query, pairs, usable)
    mixed = jnp.dot(attended.reshape(-1, model_width), w_out, preferred_element_type=jnp.float32)
    return mixed.astype(jnp.bfloat16).reshape(tokens.shape)


def solution(mesh):
    return jax.shard_map(
        on_device,
        mesh=mesh,
        in_specs=(P("lat", "lon", None, None), P(), P(), P("lat", "lon", None)),
        out_specs=P("lat", "lon", None, None),
        check_vma=False,
    )
```

profile of v0, /device:TPU:1, one launch (start us, length us, event | category | flops | bytes accessed | tf_op | source)
XLA Modules:
  0.0 397.0 jit_solution(2091455208403304675)
XLA Ops:
  6.5 4.9 %convolution_convert_fusion = bf16[256,3072]{1,0:T(8,128)(2,1)S(1)} fusion(bf16[256,1024]{1,0:T(8,128)(2,1)} %bitcast.128, bf16[1024,3072]{1,0:T(8,128)(2,1)} %param.8), kind=kOutput, calls=%fused_computation.21 | convolution fusion | flops 1611399168 | bytes 8388608 | tf_op jit(solution)/shard_map/dot_general | solution.py:76
  15.0 3.8 collective-permute-start
  18.8 5.4 %collective-permute-start.1 = (bf16[1,1,128,2048]{3,2,1,0:T(8,128)(2,1)S(1)}, bf16[1,1,128,2048]{3,2,1,0:T(8,128)(2,1)S(1)}, u32[]{:S(2)}, u32[]{:S(2)}) collective-permute-start(bf16[1,1,128,2048]{3,2,1,0:T(8,128)(2,1)S(1)} %get-tuple-element.131), channel_id=1, source_target_pairs={{1,0},{2,1},{3,2},{4,3},{5,4},{6,5},{7,6},{8,7},{9,8},{10,9},{11,1... | collective-permute-start | bytes 1572872 | tf_op jit(solution)/shard_map/ppermute | solution.py:19
  24.2 24.0 %collective-permute-done = bf16[1,1,128,2048]{3,2,1,0:T(8,128)(2,1)S(1)} collective-permute-done((bf16[1,1,128,2048]{3,2,1,0:T(8,128)(2,1)S(1)}, bf16[1,1,128,2048]{3,2,1,0:T(8,128)(2,1)S(1)}, u32[]{:S(2)}, u32[]{:S(2)}) %collective-permute-start) | collective-permute-done | bytes 524320 | tf_op jit(solution)/shard_map/ppermute | solution.py:18
  48.2 3.2 collective-permute-done.1
  51.4 3.0 pad_maximum_fusion
  54.4 7.0 %collective-permute-start.2 = (bf16[1,4,128,2048]{3,2,1,0:T(8,128)(2,1)}, bf16[1,4,128,2048]{3,2,1,0:T(8,128)(2,1)}, u32[]{:S(2)}, u32[]{:S(2)}) collective-permute-start(bf16[1,4,128,2048]{3,2,1,0:T(8,128)(2,1)} %pad_maximum_fusion), channel_id=1, source_target_pairs={{0,16},{16,32},{32,48},{48,64},{64,80},{80,96},{96,112},{112,128},... | collective-permute-start | bytes 6291464 | tf_op jit(solution)/shard_map/ppermute | solution.py:18
  66.0 55.3 %collective-permute-done.2 = bf16[1,4,128,2048]{3,2,1,0:T(8,128)(2,1)} collective-permute-done((bf16[1,4,128,2048]{3,2,1,0:T(8,128)(2,1)}, bf16[1,4,128,2048]{3,2,1,0:T(8,128)(2,1)}, u32[]{:S(2)}, u32[]{:S(2)}) %collective-permute-start.2) | collective-permute-done | bytes 2097184 | tf_op jit(solution)/shard_map/ppermute | solution.py:18
  134.9 127.6 %all-gather.2.cloned.1.call-done = bf16[1,32,128,2048]{3,2,0,1:T(8,128)(2,1)} async-done(((bf16[1,2,128,2048]{3,2,0,1:T(8,128)(2,1)}), bf16[1,32,128,2048]{3,2,0,1:T(8,128)(2,1)}) %all-gather.2.cloned.1.call-update) | async-done | bytes 16777232 | tf_op jit(solution)/shard_map/all_gather | solution.py:63
  262.5 10.7 %gather_fusion = bf16[16,128,2048]{2,1,0:T(8,128)(2,1)} fusion(bf16[1,32,128,2048]{3,2,0,1:T(8,128)(2,1)} %all-gather.2.cloned.1.call-done, s32[16]{0:T(128)S(1)} %or_bitcast_fusion), kind=kCustom, calls=%fused_computation | custom fusion | bytes 16777344 | tf_op jit(solution)/shard_map/vmap(jit(_take))/gather | solution.py:55
  273.2 10.4 %select_dynamic-update-slice_fusion = bf16[1,2,17,128,2048]{4,3,2,1,0:T(8,128)(2,1)} fusion(bf16[1,2,17,128,2048]{4,3,2,1,0:T(8,128)(2,1)} %fusion.16, bf16[1,2,8,128,2048]{4,3,2,1,0:T(8,128)(2,1)} %bitcast.118, pred[2,8]{1,0:T(4,128)(4,1)S(1)} %compare_and_fusion, pred[2,8]{1,0:T(4,128)(4,1)S(1)} %and_bitcast_fusion.1), kind=kLoop, calls=%fused_computation.20 | loop fusion | flops 8388608 | bytes 16777248 | tf_op jit(solution)/shard_map/concatenate | solution.py:91
  283.6 22.2 %copy.37 = bf16[2,2176,2048]{1,2,0:T(8,128)(2,1)} copy(bf16[2,2176,2048]{2,1,0:T(8,128)(2,1)} %bitcast.25) | data formatting | bytes 35651584
  305.8 81.5 %while.13 = (s32[]{:T(128)}, bf16[8,2,128,128]{2,3,1,0:T(8,128)(2,1)}, s32[8]{0:T(128)S(1)}, bf16[2,2176,2048]{1,2,0:T(8,128)(2,1)}, bf16[2,128,1024]{2,1,0:T(8,...) while((s32[]{:T(128)}, ...), condition=%wide.region_3.4_spmd.clone, body=%wide.region_0.0_spmd.clone.sunk | while | flops 437883648 | bytes 8397814 | solution.py:50
  312.3 3.1 fusion.51
  317.3 2.8 constant_dynamic-slice_fusion.5
  322.5 3.1 fusion.51
  327.4 2.8 constant_dynamic-slice_fusion.5
  332.7 3.1 fusion.51
  337.6 2.8 constant_dynamic-slice_fusion.5
  342.9 3.1 fusion.51
  353.0 3.1 fusion.51
  363.2 3.1 fusion.51
  373.4 3.1 fusion.51
  383.6 3.1 fusion.51
  (93 shorter events, 67.9 us)
Async XLA Ops:
  6.5 382.1 %copy-start = (bf16[1024,1024]{1,0:T(8,128)(2,1)S(1)}, bf16[1024,1024]{1,0:T(8,128)(2,1)}, u32[]{:S(2)}) copy-start(bf16[1024,1024]{1,0:T(8,128)(2,1)} %param.9) | copy-start | bytes 6291460
  6.5 256.0 %all-gather.2.cloned.1.call-start = ((), (), s32[]{:S(2)}) async-start(), calls=%async_computation | async-start | bytes 17825792 | tf_op jit(solution)/shard_map/all_gather | solution.py:63
  11.4 1.2 copy-start.6
  13.7 49.6 %copy-start.7 = (s32[1,2,8]{2,1,0:T(2,128)S(1)}, s32[1,2,8]{2,1,0:T(2,128)}, u32[]{:S(2)}) copy-start(s32[1,2,8]{2,1,0:T(2,128)} %param.10) | copy-start | bytes 196
  13.7 49.7 %copy-start.8 = (s32[9]{0:T(128)S(1)}, s32[9]{0:T(128)}, u32[]{:S(2)}) copy-start(s32[9]{0:T(128)} %constant.95.clone) | copy-start | bytes 112
  15.0 33.2 %collective-permute-start = (bf16[1,1,128,2048]{3,2,1,0:T(8,128)(2,1)S(1)}, bf16[1,1,128,2048]{3,2,1,0:T(8,128)(2,1)S(1)}, u32[]{:S(2)}, u32[]{:S(2)}) collective-permute-start(bf16[1,1,128,2048]{3,2,1,0:T(8,128)(2,1)S(1)} %get-tuple-element.130), channel_id=1, source_target_pairs={{0,1},{1,2},{2,3},{3,4},{4,5},{5,6},{6,7},{7,8},{8,9},{9,10},{10,1... | collective-permute-start | bytes 1572872 | tf_op jit(solution)/shard_map/ppermute | solution.py:18
  18.8 32.6 %collective-permute-start.1 = (bf16[1,1,128,2048]{3,2,1,0:T(8,128)(2,1)S(1)}, bf16[1,1,128,2048]{3,2,1,0:T(8,128)(2,1)S(1)}, u32[]{:S(2)}, u32[]{:S(2)}) collective-permute-start(bf16[1,1,128,2048]{3,2,1,0:T(8,128)(2,1)S(1)} %get-tuple-element.131), channel_id=1, source_target_pairs={{1,0},{2,1},{3,2},{4,3},{5,4},{6,5},{7,6},{8,7},{9,8},{10,9},{11,1... | collective-permute-start | bytes 1572872 | tf_op jit(solution)/shard_map/ppermute | solution.py:19
  48.2 3.2 copy-start.2
  51.4 3.0 copy-start.4
  54.4 74.0 %copy-start.1 = (bf16[256,2048]{1,0:T(8,128)(2,1)S(1)}, bf16[256,2048]{1,0:T(8,128)(2,1)}, u32[]{:S(2)}) copy-start(bf16[256,2048]{1,0:T(8,128)(2,1)} %slice.52) | copy-start | bytes 3145732
  54.4 66.9 %collective-permute-start.2 = (bf16[1,4,128,2048]{3,2,1,0:T(8,128)(2,1)}, bf16[1,4,128,2048]{3,2,1,0:T(8,128)(2,1)}, u32[]{:S(2)}, u32[]{:S(2)}) collective-permute-start(bf16[1,4,128,2048]{3,2,1,0:T(8,128)(2,1)} %pad_maximum_fusion), channel_id=1, source_target_pairs={{0,16},{16,32},{32,48},{48,64},{64,80},{80,96},{96,112},{112,128},... | collective-permute-start | bytes 6291464 | tf_op jit(solution)/shard_map/ppermute | solution.py:18
  63.4 65.1 %copy-start.3 = (bf16[1,1,128,2048]{3,2,1,0:T(8,128)(2,1)S(1)}, bf16[1,1,128,2048]{3,2,1,0:T(8,128)(2,1)}, u32[]{:S(2)}) copy-start(bf16[1,1,128,2048]{3,2,1,0:T(8,128)(2,1)} %copy-done.2) | copy-start | bytes 1572868
  63.5 68.1 %collective-permute-start.3 = (bf16[1,4,128,2048]{3,2,1,0:T(8,128)(2,1)}, bf16[1,4,128,2048]{3,2,1,0:T(8,128)(2,1)S(1)}, u32[]{:S(2)}, u32[]{:S(2)}) collective-permute-start(bf16[1,4,128,2048]{3,2,1,0:T(8,128)(2,1)} %pad_maximum_fusion), channel_id=1, source_target_pairs={{16,0},{32,16},{48,32},{64,48},{80,64},{96,80},{112,96},{128,112},... | collective-permute-start | bytes 6291464 | tf_op jit(solution)/shard_map/ppermute | solution.py:19
  123.7 6.8 %copy-start.5 = (bf16[1,1,128,2048]{3,2,1,0:T(8,128)(2,1)S(1)}, bf16[1,1,128,2048]{3,2,1,0:T(8,128)(2,1)}, u32[]{:S(2)}) copy-start(bf16[1,1,128,2048]{3,2,1,0:T(8,128)(2,1)} %copy-done.4) | copy-start | bytes 1572868
Sparse Core Ops, SparseCore 0:
  13.8 248.6 all-gather.1
where the time goes:
time: 399 us; the launch traced here: 397 us
  waiting for transfers between devices  210 us (53%)
  local copies, waits for them, and re-layouts  91.2 us (23%)
  matrix products  42.5 us (11%)
  starting transfers between devices  18.7 us (5%)
  other arithmetic  15.6 us (4%)
  between operations  13.5 us (3%)
  loops' own time  5.31 us (1%)
    all_gather x1, waiting for transfers between devices, fetch_far(): piece = lax.all_gather(material, 'lon', axis=1, tiled=True)  128 us
    ppermute x2, waiting for transfers between devices, padded_2(): before = lax.ppermute(last, axis, up)  79.4 us
    unnamed x26, local copies, waits for them, and re-layouts  34.8 us
    dot_general x8, matrix products, one_group(): jnp.einsum('thqk,tkhd->tqhd', weights, value_part, preferred_element_type...  24.4 us
    dynamic_slice x8, local copies, waits for them, and re-layouts, one_group(): key_part = lax.dynamic_slice_in_dim(pairs, column_start, group_width, 2)  22.4 us
    sub x8, matrix products, one_group(): expos = jnp.exp(scores - peak)  11.7 us
    ppermute x2, starting transfers between devices, padded_2(): before = lax.ppermute(last, axis, up)  10.8 us
    gather x2, local copies, waits for them, and re-layouts, take_row(): return jnp.take(panel_row, index_row, axis=0)  10.7 us
  transfers between devices with their start and end apart: 5, of which 4 were waited for; matrix products, arithmetic and copies ran while one was open for 5% of the time, Pallas kernels for 0%

commit v1 on v0

v1 whole, which is shorter than its diff:
```python
import functools

import jax
import jax.numpy as jnp
from jax import lax
from jax.experimental import pallas as pl
from jax.experimental.pallas import tpu as pltpu
from jax.sharding import PartitionSpec as P

MESH = pl.DeviceIdType.MESH
BF = jnp.bfloat16
F32 = jnp.float32
H = 16
HD = 64
BLOCK = 128
PAIRS = H // 2
SENDS = 36


def nt_dot(a, b):
    return lax.dot_general(a, b, (((1,), (1,)), ((), ())), preferred_element_type=F32)


def nn_dot(a, b):
    return jnp.dot(a, b, preferred_element_type=F32)


def layer_kernel(
    comm,
    compute,
    ids,
    tok,
    wqkv,
    wout,
    out,
    g,
    nb,
    wq,
    wvt,
    wo,
    x,
    kn,
    vn,
    kt,
    vt,
    qmt,
    ms,
    ls,
    acc,
    att,
    send_sem,
    g_sem,
    n_sem,
    load_sem,
):
    n_lat, n_lon = lax.axis_size("lat"), lax.axis_size("lon")
    n_z = n_lon // 2
    width = wo.shape[0]
    lat, lon = lax.axis_index("lat"), lax.axis_index("lon")
    z, y_hi = lon // 2, lon % 2
    core = lat % 2
    sign = 1 - 2 * core

    def at(step, line):
        return lax.rem(z + step + n_z, n_z) * 2 + (y_hi if line == 0 else 1 - y_hi)

    partner = at(0, 1)
    lat_chip = lat + sign
    lat_off = lax.rem(lat + n_lat - sign, n_lat)
    lon_left, lon_right = lax.rem(lon + n_lon - 1, n_lon), lax.rem(lon + 1, n_lon)
    off_inside = jnp.where(core == 0, lat > 0, lat < n_lat - 1)

    loads = [
        pltpu.make_async_copy(tok, g.at[lon], load_sem.at[0]),
        pltpu.make_async_copy(wqkv, wq, load_sem.at[1]),
        pltpu.make_async_copy(wout, wo, load_sem.at[2]),
    ]
    for load in loads:
        load.start()

    sends = []

    def send(src, dst, sem, dev):
        if comm:
            copy = pltpu.make_async_remote_copy(
                src_ref=src,
                dst_ref=dst,
                send_sem=send_sem.at[len(sends)],
                recv_sem=sem,
                device_id=dev,
                device_id_type=MESH,
            )
            copy.start()
            sends.append(copy)

    def arrived(ref, sem):
        if comm:
            pltpu.make_async_remote_copy(
                src_ref=ref,
                dst_ref=ref,
                send_sem=send_sem.at[0],
                recv_sem=sem,
                device_id=(lat, partner),
                device_id_type=MESH,
            ).wait_recv()

    def send_g(owner, col, dev):
        send(g.at[owner, col], g.at[owner, col], g_sem.at[owner, col], dev)

    def wait_g(owner, col):
        arrived(g.at[owner, col], g_sem.at[owner, col])

    if comm:
        barrier = pltpu.get_barrier_semaphore()
        friends = [
            (lat, at(1, 0)),
            (lat, at(-1, 0)),
            (lat, partner),
            (lat_chip, lon),
            (lat_off, lon),
            (lat_off, lon_left),
            (lat_off, lon_right),
        ]
        for friend in friends:
            pl.semaphore_signal(barrier, inc=1, device_id=friend, device_id_type=MESH)
        pl.semaphore_wait(barrier, len(friends))

    up, down = (lat, at(1, 0)), (lat, at(-1, 0))
    across = (lat, partner)

    def send_own(col, dev):
        send(tok.at[col], g.at[lon, col], g_sem.at[lon, col], dev)

    send_own(0, across)
    send_own(1, up)
    send_own(1, down)
    send_own(0, up)
    send_own(0, down)
    send(tok, nb.at[0, pl.ds(1, 2)], n_sem.at[0, 0], (lat_chip, lon))
    send(tok, nb.at[1, pl.ds(1, 2)], n_sem.at[1, 0], (lat_off, lon))
    send(tok.at[0], nb.at[1, 3], n_sem.at[1, 2], (lat_off, lon_left))
    send(tok.at[1], nb.at[1, 0], n_sem.at[1, 1], (lat_off, lon_right))
    send_own(1, across)

    def lookup(owner):
        col = jnp.int32(0)
        which = jnp.int32(0)
        for entry in range(16):
            value = ids[entry]
            hit = lax.shift_right_logical(value, 1) == owner
            col = jnp.where(hit, value & 1, col)
            which = jnp.where(hit, jnp.int32(entry // 8), which)
        return col, which

    def project(source, k_dst, v_dst):
        @pl.loop(0, width // 256)
        def _(step):
            cols = pl.ds(pl.multiple_of(step * 256, 256), 256)
            k_cols = pl.ds(pl.multiple_of(width + step * 256, 256), 256)
            k_dst[:, cols] = nn_dot(source[...], wq[:, k_cols]).astype(BF)
            v_dst[cols, :] = nt_dot(wvt[cols, :], source[...]).astype(BF)

    def pair_cols(pair):
        return pl.ds(pl.multiple_of(pair * 128, 128), 128)

    def merge(pair, j, scores, values, first):
        peak = jnp.max(scores[0], axis=0, keepdims=True)
        for s in scores[1:]:
            peak = jnp.maximum(peak, jnp.max(s, axis=0, keepdims=True))
        if not first:
            before = ms[j, pair]
            peak = jnp.maximum(peak, before)
        total = None
        summed = None
        for s, v in zip(scores, values):
            expos = jnp.exp(s - peak)
            part = jnp.sum(expos, axis=0, keepdims=True)
            prod = nn_dot(v, expos.astype(BF))
            total = part if total is None else total + part
            summed = prod if summed is None else summed + prod
        even, odd = summed[:HD, :BLOCK], summed[HD:, BLOCK:]
        if not first:
            decay = jnp.exp(before - peak)
            total = total + ls[j, pair] * decay
            even = even + acc[j, pair, 0] * decay[:, :BLOCK]
            odd = odd + acc[j, pair, 1] * decay[:, BLOCK:]
        ms[j, pair] = peak
        ls[j, pair] = total
        acc[j, pair, 0] = even
        acc[j, pair, 1] = odd

    def near(keys_of, first):
        @pl.loop(0, PAIRS)
        def _(pair):
            cols = pair_cols(pair)
            for j in range(2):
                queries = qmt[j, pair]
                scores, values = [], []
                for row, start, size in keys_of(j):
                    scores.append(nn_dot(kn[row, pl.ds(start, size), cols], queries))
                    values.append(vn[row, cols, pl.ds(start, size)])
                merge(pair, j, scores, values, first)

    def far(owners):
        count = len(owners)
        whiches = []
        for i, owner in enumerate(owners):
            col, which = lookup(owner)
            whiches.append(which)
            x[i * BLOCK : (i + 1) * BLOCK] = jnp.where(col == 1, g[owner, 1], g[owner, 0])
        rows = pl.ds(0, count * BLOCK)
        project(x.at[rows], kt.at[rows], vt.at[:, rows])

        @pl.loop(0, PAIRS)
        def _(pair):
            cols = pair_cols(pair)
            scores = []
            peaks = []
            for i in range(count):
                s = nn_dot(kt[i * BLOCK : (i + 1) * BLOCK, cols], qmt[whiches[i], pair])
                scores.append(s)
                peaks.append(jnp.max(s, axis=0, keepdims=True))
            before = [ms[j, pair] for j in range(2)]
            now = []
            for j in range(2):
                peak = before[j]
                for i in range(count):
                    peak = jnp.maximum(peak, jnp.where(whiches[i] == j, peaks[i], before[j]))
                now.append(peak)
            decay = [jnp.exp(before[j] - now[j]) for j in range(2)]
            totals = [ls[j, pair] * decay[j] for j in range(2)]
            evens = [acc[j, pair, 0] * decay[j][:, :BLOCK] for j in range(2)]
            odds = [acc[j, pair, 1] * decay[j][:, BLOCK:] for j in range(2)]
            for i in range(count):
                expos = jnp.exp(scores[i] - jnp.where(whiches[i] == 0, now[0], now[1]))
                part = jnp.sum(expos, axis=0, keepdims=True)
                prod = nn_dot(vt[cols, i * BLOCK : (i + 1) * BLOCK], expos.astype(BF))
                even, odd = prod[:HD, :BLOCK], prod[HD:, BLOCK:]
                for j in range(2):
                    mine = whiches[i] == j
                    totals[j] = totals[j] + jnp.where(mine, part, 0.0)
                    evens[j] = evens[j] + jnp.where(mine, even, 0.0)
                    odds[j] = odds[j] + jnp.where(mine, odd, 0.0)
            for j in range(2):
                ms[j, pair] = now[j]
                ls[j, pair] = totals[j]
                acc[j, pair, 0] = evens[j]
                acc[j, pair, 1] = odds[j]

    def own_projection():
        own = g.at[lon]

        @pl.loop(0, width // 128)
        def _(step):
            cols = pl.ds(pl.multiple_of(step * 128, 128), 128)
            v_cols = pl.ds(pl.multiple_of(2 * width + step * 128, 128), 128)
            wvt[cols, :] = wq[:, v_cols].T

        @pl.loop(0, width // 256)
        def _(step):
            cols = pl.ds(pl.multiple_of(step * 256, 256), 256)
            tokens = own[...].reshape(2 * BLOCK, width)
            queries = nn_dot(tokens, wq[:, cols]).astype(BF).astype(F32) * HD**-0.5
            row = lax.broadcasted_iota(jnp.int32, (BLOCK, BLOCK), 0)
            for j in range(2):
                for half in range(2):
                    block = queries[j * BLOCK : (j + 1) * BLOCK, half * 128 : (half + 1) * 128].T
                    even = jnp.where(row < HD, block, 0.0)
                    odd = jnp.where(row < HD, 0.0, block)
                    qmt[j, step * 2 + half] = jnp.concatenate([even, odd], axis=1).astype(BF)
        x[: 2 * BLOCK] = own[...].reshape(2 * BLOCK, width)
        project(x.at[pl.ds(0, 256)], kn.at[0, pl.ds(128, 256)], vn.at[0, :, pl.ds(128, 256)])

    def finish():
        @pl.loop(0, PAIRS)
        def _(pair):
            cols = pair_cols(pair)
            for j in range(2):
                total = ls[j, pair]
                even = acc[j, pair, 0] / total[:, :BLOCK]
                odd = acc[j, pair, 1] / total[:, BLOCK:]
                att[j * BLOCK : (j + 1) * BLOCK, cols] = jnp.concatenate([even, odd], axis=0).T.astype(BF)

        @pl.loop(0, width // 256)
        def _(step):
            cols = pl.ds(pl.multiple_of(step * 256, 256), 256)
            out[:, cols] = nn_dot(att[...], wo[:, cols]).astype(BF)

    for load in loads:
        load.wait()
    if compute:
        own_projection()

    wait_g(partner, 0)
    send_g(partner, 0, up)
    send_g(partner, 0, down)

    def relay(step):
        for line, col in ((0, 1), (0, 0), (1, 0)):
            low, high = at(-step, line), at(step, line)
            wait_g(low, col)
            wait_g(high, col)
            if step < n_z // 2 - 1:
                send_g(low, col, up)
                send_g(high, col, down)
            else:
                last = lax.rem(z + n_z - step * sign, n_z) * 2 + (y_hi if line == 0 else 1 - y_hi)
                send_g(last, col, (lat, lax.rem(z + n_z + sign, n_z) * 2 + y_hi))
            if line == 0 and col == 1:
                send_g(low, 1, across)
                send_g(high, 1, across)

    arrived(nb.at[0, pl.ds(1, 2)], n_sem.at[0, 0])
    if compute:
        x[: 2 * BLOCK] = nb[0, 1:3].reshape(2 * BLOCK, width)
        project(x.at[pl.ds(0, 256)], kn.at[1, pl.ds(128, 256)], vn.at[1, :, pl.ds(128, 256)])
        near(lambda j: ((0, 128, 256), (1, 128, 256)), True)

    relay(1)

    arrived(nb.at[1, pl.ds(1, 2)], n_sem.at[1, 0])
    arrived(nb.at[1, 0], n_sem.at[1, 1])
    arrived(nb.at[1, 3], n_sem.at[1, 2])
    if compute:
        @pl.when(off_inside)
        def _():
            x[...] = nb[1].reshape(4 * BLOCK, width)
            project(x, kn.at[2], vn.at[2])
            near(lambda j: ((2, j * BLOCK, 3 * BLOCK),), False)

    wait_g(partner, 1)
    wait_g(at(-1, 1), 1)
    wait_g(at(1, 1), 1)
    send(g.at[lon_left, 1], nb.at[0, 0], n_sem.at[0, 1], (lat_chip, lon))
    send(g.at[lon_right, 0], nb.at[0, 3], n_sem.at[0, 2], (lat_chip, lon))
    if compute:
        far([at(-1, 0), at(1, 0), at(-1, 1), at(1, 1)])

    relay(2)

    arrived(nb.at[0, 0], n_sem.at[0, 1])
    arrived(nb.at[0, 3], n_sem.at[0, 2])
    if compute:
        x[0:128] = g[lon_left, 1]
        x[128:256] = g[lon_right, 0]
        x[256:384] = nb[0, 0]
        x[384:512] = nb[0, 3]
        project(x, kt, vt)
        for i, (row, start) in enumerate(((0, 0), (0, 384), (1, 0), (1, 384))):
            kn[row, start : start + BLOCK] = kt[i * BLOCK : (i + 1) * BLOCK]
            vn[row, :, start : start + BLOCK] = vt[:, i * BLOCK : (i + 1) * BLOCK]
        near(lambda j: ((0, j * 384, BLOCK), (1, j * 384, BLOCK)), False)
        far([lon, partner])

    wait_g(at(-2, 1), 1)
    wait_g(at(2, 1), 1)
    if compute:
        far([at(-2, 0), at(2, 0), at(-2, 1), at(2, 1)])

    relay(3)

    wait_g(at(-3, 1), 1)
    wait_g(at(3, 1), 1)
    if compute:
        far([at(-3, 0), at(3, 0), at(-3, 1), at(3, 1)])

    wait_g(at(4, 0), 1)
    send_g(at(4, 0), 1, across)
    wait_g(at(4, 0), 0)
    wait_g(at(4, 1), 0)
    wait_g(at(4, 1), 1)
    if compute:
        far([at(4, 0), at(4, 1)])
        finish()
    else:
        out[...] = g[lon].reshape(out.shape)
    for copy in sends:
        copy.wait_send()


def on_device(tokens, w_qkv, w_out, tele_ids, comm=True, compute=True):
    shape = tokens.shape
    width = shape[3]
    tokens = tokens.reshape(2, BLOCK, width)
    n_lon = lax.axis_size("lon")
    anywhere = pl.BlockSpec(memory_space=pl.ANY)
    mixed = pl.pallas_call(
        functools.partial(layer_kernel, comm, compute),
        out_shape=jax.ShapeDtypeStruct((2 * BLOCK, width), BF),
        in_specs=[pl.BlockSpec(memory_space=pltpu.SMEM), anywhere, anywhere, anywhere],
        out_specs=pl.BlockSpec(memory_space=pltpu.VMEM),
        scratch_shapes=[
            pltpu.VMEM((n_lon, 2, BLOCK, width), BF),
            pltpu.VMEM((2, 4, BLOCK, width), BF),
            pltpu.VMEM((width, 3 * width), BF),
            pltpu.VMEM((width, width), BF),
            pltpu.VMEM((width, width), BF),
            pltpu.VMEM((4 * BLOCK, width), BF),
            pltpu.VMEM((3, 4 * BLOCK, width), BF),
            pltpu.VMEM((3, width, 4 * BLOCK), BF),
            pltpu.VMEM((4 * BLOCK, width), BF),
            pltpu.VMEM((width, 4 * BLOCK), BF),
            pltpu.VMEM((2, PAIRS, 2 * HD, 2 * BLOCK), BF),
            pltpu.VMEM((2, PAIRS, 1, 2 * BLOCK), F32),
            pltpu.VMEM((2, PAIRS, 1, 2 * BLOCK), F32),
            pltpu.VMEM((2, PAIRS, 2, HD, BLOCK), F32),
            pltpu.VMEM((2 * BLOCK, width), BF),
            pltpu.SemaphoreType.DMA((SENDS,)),
            pltpu.SemaphoreType.DMA((n_lon, 2)),
            pltpu.SemaphoreType.DMA((2, 3)),
            pltpu.SemaphoreType.DMA((3,)),
        ],
        compiler_params=pltpu.CompilerParams(
            collective_id=0 if comm else None, has_side_effects=True, vmem_limit_bytes=60 * 1024 * 1024
        ),
        name="layer",
    )(tele_ids.reshape(-1), tokens, w_qkv, w_out)
    return mixed.reshape(shape)


def solution(mesh):
    return jax.shard_map(
        on_device,
        mesh=mesh,
        in_specs=(P("lat", "lon", None, None), P(), P(), P("lat", "lon", None)),
        out_specs=P("lat", "lon", None, None),
        check_vma=False,
    )
```

time: 399 us -> 120 us (0.30)
  the two profiles are of different devices: /device:TPU:1 before, /device:TPU:12 now
where the time goes in v1:
time: 120 us
  Pallas kernels  117 us (98%)
  local copies, waits for them, and re-layouts  3.14 us (3%)
    pallas_call x1, Pallas kernels, on_device(): pl.pallas_call(functools.partial(layer_kernel, comm, compute), out_shape=...  117 us

profile of v1, /device:TPU:12, one launch (start us, length us, event | category | flops | bytes accessed | tf_op | source)
XLA Modules:
  0.0 120.0 jit_solution(12723028638404043557)
XLA Ops:
  0.0 1.3 %reshape.9.ids = s32[16]{0:T(128)} reshape(s32[1,2,8]{2,1,0:T(2,128)} %param.7) | data formatting | bytes 128 | tf_op jit(solution)/shard_map/reshape | solution.py:417
  1.3 116.9 %layer.1 = bf16[256,1024]{1,0:T(8,128)(2,1)} custom-call(s32[16]{0:T(128)} %reshape.9.ids, bf16[2,128,1024]{2,1,0:T(8,128)(2,1)} %bitcast.3, bf16[1024,3072]{1,0:T(8,128)(2,1)} %wqkv.1, bf16[1024,1024]{1,0:T(8,128)(2,1)} %wout.1), custom_call_target="tpu_custom_call" | custom-call | tf_op jit(solution)/shard_map/layer/pallas_call | solution.py:387
  118.2 1.9 %copy.6 = bf16[1,2,128,1024]{3,2,1,0:T(8,128)(2,1)} copy(bf16[1,2,128,1024]{3,2,1,0:T(8,128)(2,1)} %bitcast.2) | data formatting | bytes 1048576

commit v2 on v1

v2 whole, which is shorter than its diff:
```python
import functools

import jax
import jax.numpy as jnp
from jax import lax
from jax.experimental import pallas as pl
from jax.experimental.pallas import tpu as pltpu
from jax.sharding import PartitionSpec as P

MESH = pl.DeviceIdType.MESH
BF = jnp.bfloat16
F32 = jnp.float32
H = 16
HD = 64
BLOCK = 128
PAIRS = H // 2
SENDS = 40
TELE = 8
UNROLL = 2


def nt_dot(a, b):
    return lax.dot_general(a, b, (((1,), (1,)), ((), ())), preferred_element_type=F32)


def nn_dot(a, b):
    return jnp.dot(a, b, preferred_element_type=F32)


def layer_kernel(
    comm,
    compute,
    ids,
    ids_hbm,
    tok,
    wqkv,
    wout,
    out,
    g,
    nb,
    pick,
    picked,
    wq,
    wvt,
    wo,
    x,
    kn,
    vn,
    kt,
    vt,
    qmt,
    ms,
    ls,
    acc,
    att,
    sb0,
    sb1,
    pk0,
    pk1,
    ids_in,
    ids_across,
    send_sem,
    g_sem,
    n_sem,
    chip_sem,
    pick_sem,
    ids_sem,
    load_sem,
):
    n_lat, n_lon = lax.axis_size("lat"), lax.axis_size("lon")
    n_z = n_lon // 2
    width = wo.shape[0]
    lat, lon = lax.axis_index("lat"), lax.axis_index("lon")
    z, y_hi = lon // 2, lon % 2
    core = lat % 2
    sign = 1 - 2 * core

    def at(step, line):
        return lax.rem(z + step + n_z, n_z) * 2 + (y_hi if line == 0 else 1 - y_hi)

    partner = at(0, 1)
    sb, pk = (sb0, sb1), (pk0, pk1)
    lat_chip = lat + sign
    lat_off = lax.rem(lat + n_lat - sign, n_lat)
    lon_left, lon_right = lax.rem(lon + n_lon - 1, n_lon), lax.rem(lon + 1, n_lon)
    off_inside = jnp.where(core == 0, lat > 0, lat < n_lat - 1)

    loads = [
        pltpu.make_async_copy(tok, g.at[lon], load_sem.at[0]),
        pltpu.make_async_copy(wqkv, wq, load_sem.at[1]),
        pltpu.make_async_copy(wout, wo, load_sem.at[2]),
    ]
    for load in loads:
        load.start()

    sends = []

    def send(src, dst, sem, dev):
        if comm:
            copy = pltpu.make_async_remote_copy(
                src_ref=src,
                dst_ref=dst,
                send_sem=send_sem.at[len(sends)],
                recv_sem=sem,
                device_id=dev,
                device_id_type=MESH,
            )
            copy.start()
            sends.append(copy)

    def arrived(ref, sem):
        if comm:
            pltpu.make_async_remote_copy(
                src_ref=ref,
                dst_ref=ref,
                send_sem=send_sem.at[0],
                recv_sem=sem,
                device_id=(lat, partner),
                device_id_type=MESH,
            ).wait_recv()

    def send_g(owner, col, dev):
        send(g.at[owner, col], g.at[owner, col], g_sem.at[owner, col], dev)

    def wait_g(owner, col):
        arrived(g.at[owner, col], g_sem.at[owner, col])

    if comm:
        barrier = pltpu.get_barrier_semaphore()
        friends = [
            (lat, at(1, 0)),
            (lat, at(-1, 0)),
            (lat, partner),
            (lat_chip, lon),
            (lat_off, lon),
            (lat_off, lon_left),
            (lat_off, lon_right),
        ]
        for friend in friends:
            pl.semaphore_signal(barrier, inc=1, device_id=friend, device_id_type=MESH)
        pl.semaphore_wait(barrier, len(friends))

    up, down = (lat, at(1, 0)), (lat, at(-1, 0))
    across = (lat, partner)

    def send_own(col, dev):
        send(tok.at[col], g.at[lon, col], g_sem.at[lon, col], dev)

    send(ids_hbm, ids_in, ids_sem.at[0], across)
    send_own(0, across)
    send_own(1, across)
    send_own(1, up)
    send_own(1, down)
    send_own(0, up)
    send_own(0, down)
    send(tok, nb.at[pl.ds(0, 2)], n_sem.at[0], (lat_off, lon))
    send(tok.at[1], nb.at[2], n_sem.at[1], (lat_off, lon_right))
    send(tok.at[0], nb.at[3], n_sem.at[2], (lat_off, lon_left))

    def lookup(owner, table=None):
        col = jnp.int32(0)
        which = jnp.int32(0)
        for entry in range(2 * TELE):
            value = ids[entry] if table is None else table[0, entry]
            hit = lax.shift_right_logical(value, 1) == owner
            col = jnp.where(hit, value & 1, col)
            which = jnp.where(hit, jnp.int32(entry // TELE), which)
        return col, which

    def project(source, k_dst, v_dst):
        @pl.loop(0, width // 256, unroll=UNROLL)
        def _(step):
            cols = pl.ds(pl.multiple_of(step * 256, 256), 256)
            k_cols = pl.ds(pl.multiple_of(width + step * 256, 256), 256)
            k_dst[:, cols] = nn_dot(source[...], wq[:, k_cols]).astype(BF)
            v_dst[cols, :] = nt_dot(wvt[cols, :], source[...]).astype(BF)

    def pair_cols(pair):
        return pl.ds(pl.multiple_of(pair * 128, 128), 128)

    def pipelined(score, finish_pair):
        score(0, 0)

        @pl.loop(0, PAIRS // 2)
        def _(step):
            score(2 * step + 1, 1)
            finish_pair(2 * step, 0)
            score(jnp.minimum(2 * step + 2, PAIRS - 1), 0)
            finish_pair(2 * step + 1, 1)

    def near(keys_of, first):
        sizes = [size for _, _, size in keys_of(0)]
        count = sum(sizes)

        def score(pair, slot):
            cols = pair_cols(pair)
            for j in range(2):
                queries = qmt[j, pair]
                offset = j * count
                peak = None
                for row, start, size in keys_of(j):
                    s = nn_dot(kn[row, pl.ds(start, size), cols], queries)
                    sb[slot][pl.ds(offset, size)] = s
                    top = jnp.max(s, axis=0, keepdims=True)
                    peak = top if peak is None else jnp.maximum(peak, top)
                    offset += size
                pk[slot][j] = peak

        def finish_pair(pair, slot):
            cols = pair_cols(pair)
            for j in range(2):
                peak = pk[slot][j]
                if not first:
                    before = ms[j, pair]
                    peak = jnp.maximum(peak, before)
                total = None
                summed = None
                offset = j * count
                for row, start, size in keys_of(j):
                    expos = jnp.exp(sb[slot][pl.ds(offset, size)] - peak)
                    part = jnp.sum(expos, axis=0, keepdims=True)
                    prod = nn_dot(vn[row, cols, pl.ds(start, size)], expos.astype(BF))
                    total = part if total is None else total + part
                    summed = prod if summed is None else summed + prod
                    offset += size
                even, odd = summed[:HD, :BLOCK], summed[HD:, BLOCK:]
                if not first:
                    decay = jnp.exp(before - peak)
                    total = total + ls[j, pair] * decay
                    even = even + acc[j, pair, 0] * decay[:, :BLOCK]
                    odd = odd + acc[j, pair, 1] * decay[:, BLOCK:]
                ms[j, pair] = peak
                ls[j, pair] = total
                acc[j, pair, 0] = even
                acc[j, pair, 1] = odd

        pipelined(score, finish_pair)

    def far(tiles, own=False):
        whiches = []
        for i, (owner, both, one) in enumerate(tiles):
            col, which = lookup(owner)
            whiches.append(which)
            rows = slice(i * BLOCK, (i + 1) * BLOCK)
            x[rows] = one[...] if both is None else jnp.where(col == 1, both[1], both[0])
        rows = pl.ds(0, len(tiles) * BLOCK)
        project(x.at[rows], kt.at[rows], vt.at[:, rows])
        if own:
            col, which = lookup(lon)
            last = slice(len(tiles) * BLOCK, (len(tiles) + 1) * BLOCK)
            whiches.append(which)
            kt[last] = jnp.where(col == 1, kn[0, BLOCK : 2 * BLOCK], kn[0, :BLOCK])
            vt[:, last] = jnp.where(col == 1, vn[0, :, BLOCK : 2 * BLOCK], vn[0, :, :BLOCK])
        count = len(whiches)
        keys = count * BLOCK

        def score(pair, slot):
            cols = pair_cols(pair)
            for i in range(count):
                s = nn_dot(kt[i * BLOCK : (i + 1) * BLOCK, cols], qmt[whiches[i], pair])
                sb[slot][i * BLOCK : (i + 1) * BLOCK] = s
                pk[slot][i] = jnp.max(s, axis=0, keepdims=True)

        def finish_pair(pair, slot):
            cols = pair_cols(pair)
            peaks = [pk[slot][i] for i in range(count)]
            before = [ms[j, pair] for j in range(2)]
            now = []
            for j in range(2):
                peak = before[j]
                for i in range(count):
                    peak = jnp.maximum(peak, jnp.where(whiches[i] == j, peaks[i], before[j]))
                now.append(peak)
            decay = [jnp.exp(before[j] - now[j]) for j in range(2)]
            totals = [ls[j, pair] * decay[j] for j in range(2)]
            weights = [[], []]
            for i in range(count):
                mine = whiches[i] == 0
                expos = jnp.exp(sb[slot][i * BLOCK : (i + 1) * BLOCK] - jnp.where(mine, now[0], now[1]))
                part = jnp.sum(expos, axis=0, keepdims=True)
                rounded = expos.astype(BF)
                none = jnp.zeros_like(rounded)
                totals[0] = totals[0] + jnp.where(mine, part, 0.0)
                totals[1] = totals[1] + jnp.where(mine, 0.0, part)
                weights[0].append(jnp.where(mine, rounded, none))
                weights[1].append(jnp.where(mine, none, rounded))
            for j in range(2):
                summed = nn_dot(vt[cols, :keys], jnp.concatenate(weights[j], axis=0))
                ms[j, pair] = now[j]
                ls[j, pair] = totals[j]
                acc[j, pair, 0] = acc[j, pair, 0] * decay[j][:, :BLOCK] + summed[:HD, :BLOCK]
                acc[j, pair, 1] = acc[j, pair, 1] * decay[j][:, BLOCK:] + summed[HD:, BLOCK:]

        pipelined(score, finish_pair)

    def own_projection():
        own = g.at[lon]

        @pl.loop(0, width // 128)
        def _(step):
            cols = pl.ds(pl.multiple_of(step * 128, 128), 128)
            v_cols = pl.ds(pl.multiple_of(2 * width + step * 128, 128), 128)
            wvt[cols, :] = wq[:, v_cols].T

        @pl.loop(0, width // 256)
        def _(step):
            cols = pl.ds(pl.multiple_of(step * 256, 256), 256)
            tokens = own[...].reshape(2 * BLOCK, width)
            queries = nn_dot(tokens, wq[:, cols]).astype(BF).astype(F32) * HD**-0.5
            row = lax.broadcasted_iota(jnp.int32, (BLOCK, BLOCK), 0)
            for j in range(2):
                for half in range(2):
                    block = queries[j * BLOCK : (j + 1) * BLOCK, half * 128 : (half + 1) * 128].T
                    even = jnp.where(row < HD, block, 0.0)
                    odd = jnp.where(row < HD, 0.0, block)
                    qmt[j, step * 2 + half] = jnp.concatenate([even, odd], axis=1).astype(BF)
        x[: 2 * BLOCK] = own[...].reshape(2 * BLOCK, width)
        project(x.at[pl.ds(0, 256)], kn.at[0, pl.ds(0, 256)], vn.at[0, :, pl.ds(0, 256)])

    def finish():
        @pl.loop(0, PAIRS)
        def _(pair):
            cols = pair_cols(pair)
            for j in range(2):
                total = ls[j, pair]
                even = acc[j, pair, 0] / total[:, :BLOCK]
                odd = acc[j, pair, 1] / total[:, BLOCK:]
                att[j * BLOCK : (j + 1) * BLOCK, cols] = jnp.concatenate([even, odd], axis=0).T.astype(BF)

        @pl.loop(0, width // 256)
        def _(step):
            cols = pl.ds(pl.multiple_of(step * 256, 256), 256)
            out[:, cols] = nn_dot(att[...], wo[:, cols]).astype(BF)

    def onward(owner, col, direction):
        send_g(owner, col, up if direction > 0 else down)

    def relay(step, col):
        wait_g(at(-step, 0), col)
        wait_g(at(step, 0), col)
        onward(at(-step, 0), col, 1)
        onward(at(step, 0), col, -1)

    def select(slot, owner):
        if comm:
            col, _ = lookup(owner, ids_across)
            pick[slot] = jnp.where(col == 1, g[owner, 1], g[owner, 0])

    def hand(slot):
        send(pick.at[slot], picked.at[slot], pick_sem.at[slot], across)

    def given(slot):
        arrived(picked.at[slot], pick_sem.at[slot])

    def both(step, line):
        owner = at(step, line)
        return owner, g.at[owner], None

    def single(step, slot):
        return at(step, 1), None, picked.at[slot]

    for load in loads:
        load.wait()
    if compute:
        own_projection()

    relay(1, 1)
    chip = (lat_chip, lon)
    send(kn.at[0, pl.ds(0, 256)], kn.at[1, pl.ds(0, 256)], chip_sem.at[0], chip)
    send(vn.at[0, :, pl.ds(0, 256)], vn.at[1, :, pl.ds(0, 256)], chip_sem.at[1], chip)
    if comm:
        arrived(ids_in, ids_sem.at[0])
        table = pltpu.make_async_copy(ids_in, ids_across, ids_sem.at[1])
        table.start()
        table.wait()
    relay(1, 0)
    arrived(kn.at[1, pl.ds(0, 256)], chip_sem.at[0])
    arrived(vn.at[1, :, pl.ds(0, 256)], chip_sem.at[1])
    if compute:
        near(lambda j: ((0, 0, 256), (1, 0, 256)), True)

    wait_g(partner, 0)
    wait_g(partner, 1)
    turn = 1 - 2 * y_hi
    ahead = (lat, lax.rem(z + turn + n_z, n_z) * 2 + y_hi)
    behind = (lat, lax.rem(z - turn + n_z, n_z) * 2 + y_hi)
    send_g(partner, 1 - y_hi, ahead)
    if compute:
        far([both(0, 1), both(-1, 0), both(1, 0)], own=True)

    relay(2, 1)
    relay(2, 0)
    select(0, at(-2, 0))
    select(1, at(2, 0))
    wait_g(lax.rem(z - turn + n_z, n_z) * 2 + 1 - y_hi, 1 - y_hi)
    if compute:
        x[0:128] = g[lon_left, 1]
        x[128:256] = g[lon_right, 0]
        project(x.at[pl.ds(0, 256)], kn.at[0, pl.ds(256, 256)], vn.at[0, :, pl.ds(256, 256)])
    hand(0)
    hand(1)
    send(kn.at[0, pl.ds(256, 256)], kn.at[1, pl.ds(256, 256)], chip_sem.at[2], chip)
    send(vn.at[0, :, pl.ds(256, 256)], vn.at[1, :, pl.ds(256, 256)], chip_sem.at[3], chip)

    arrived(nb.at[pl.ds(0, 2)], n_sem.at[0])
    arrived(nb.at[2], n_sem.at[1])
    arrived(nb.at[3], n_sem.at[2])
    if compute:
        @pl.when(off_inside)
        def _():
            project(nb.reshape(4 * BLOCK, width), kn.at[2], vn.at[2])
            near(lambda j: ((2, 0, 256), (2, 256 + j * BLOCK, BLOCK)), False)

    wait_g(at(-3, 0), 1)
    wait_g(at(3, 0), 1)
    wait_g(at(-3, 0), 0)
    wait_g(at(3, 0), 0)
    last = lax.rem(z + n_z - 3 * sign, n_z) * 2 + y_hi
    beyond = (lat, lax.rem(z + n_z + sign, n_z) * 2 + y_hi)
    send_g(last, 1, beyond)
    send_g(last, 0, beyond)
    select(2, at(-3, 0))
    select(3, at(3, 0))
    send_g(partner, 1 - y_hi, behind)
    send_g(partner, y_hi, ahead)
    send_g(partner, y_hi, behind)
    hand(2)
    hand(3)

    arrived(kn.at[1, pl.ds(256, 256)], chip_sem.at[2])
    arrived(vn.at[1, :, pl.ds(256, 256)], chip_sem.at[3])
    if compute:
        near(lambda j: ((0, 256 + j * BLOCK, BLOCK), (1, 256 + j * BLOCK, BLOCK)), False)

    given(0)
    given(1)
    if compute:
        far([both(-2, 0), both(2, 0), single(-2, 0), single(2, 1)])

    wait_g(at(4, 0), 1)
    wait_g(at(4, 0), 0)
    select(4, at(4, 0))
    hand(4)
    if compute:
        far([both(-3, 0), both(3, 0), both(4, 0)])

    given(2)
    given(3)
    wait_g(lax.rem(z + turn + n_z, n_z) * 2 + 1 - y_hi, 1 - y_hi)
    wait_g(at(-1, 1), y_hi)
    wait_g(at(1, 1), y_hi)
    if compute:
        far([both(-1, 1), both(1, 1), single(-3, 2), single(3, 3)])
    given(4)
    if compute:
        far([single(4, 4)])
        finish()
    else:
        out[...] = g[lon].reshape(out.shape)
    for copy in sends:
        copy.wait_send()


def on_device(tokens, w_qkv, w_out, tele_ids, comm=True, compute=True):
    shape = tokens.shape
    width = shape[3]
    tokens = tokens.reshape(2, BLOCK, width)
    n_lon = lax.axis_size("lon")
    anywhere = pl.BlockSpec(memory_space=pl.ANY)
    mixed = pl.pallas_call(
        functools.partial(layer_kernel, comm, compute),
        out_shape=jax.ShapeDtypeStruct((2 * BLOCK, width), BF),
        in_specs=[pl.BlockSpec(memory_space=pltpu.SMEM)] + [anywhere] * 4,
        out_specs=pl.BlockSpec(memory_space=pltpu.VMEM),
        scratch_shapes=[
            pltpu.VMEM((n_lon, 2, BLOCK, width), BF),
            pltpu.VMEM((4, BLOCK, width), BF),
            pltpu.VMEM((5, BLOCK, width), BF),
            pltpu.VMEM((5, BLOCK, width), BF),
            pltpu.VMEM((width, 3 * width), BF),
            pltpu.VMEM((width, width), BF),
            pltpu.VMEM((width, width), BF),
            pltpu.VMEM((4 * BLOCK, width), BF),
            pltpu.VMEM((3, 4 * BLOCK, width), BF),
            pltpu.VMEM((3, width, 4 * BLOCK), BF),
            pltpu.VMEM((4 * BLOCK, width), BF),
            pltpu.VMEM((width, 4 * BLOCK), BF),
            pltpu.VMEM((2, PAIRS, 2 * HD, 2 * BLOCK), BF),
            pltpu.VMEM((2, PAIRS, 1, 2 * BLOCK), F32),
            pltpu.VMEM((2, PAIRS, 1, 2 * BLOCK), F32),
            pltpu.VMEM((2, PAIRS, 2, HD, BLOCK), F32),
            pltpu.VMEM((2 * BLOCK, width), BF),
            pltpu.VMEM((8 * BLOCK, 2 * BLOCK), F32),
            pltpu.VMEM((8 * BLOCK, 2 * BLOCK), F32),
            pltpu.VMEM((4, 1, 2 * BLOCK), F32),
            pltpu.VMEM((4, 1, 2 * BLOCK), F32),
            pltpu.VMEM((1, 2 * TELE), jnp.int32),
            pltpu.SMEM((1, 2 * TELE), jnp.int32),
            pltpu.SemaphoreType.DMA((SENDS,)),
            pltpu.SemaphoreType.DMA((n_lon, 2)),
            pltpu.SemaphoreType.DMA((3,)),
            pltpu.SemaphoreType.DMA((4,)),
            pltpu.SemaphoreType.DMA((5,)),
            pltpu.SemaphoreType.DMA((2,)),
            pltpu.SemaphoreType.DMA((3,)),
        ],
        compiler_params=pltpu.CompilerParams(
            collective_id=0 if comm else None, has_side_effects=True, vmem_limit_bytes=60 * 1024 * 1024
        ),
        name="layer",
    )(tele_ids.reshape(-1), tele_ids.reshape(1, -1), tokens, w_qkv, w_out)
    return mixed.reshape(shape)


def solution(mesh):
    return jax.shard_map(
        on_device,
        mesh=mesh,
        in_specs=(P("lat", "lon", None, None), P(), P(), P("lat", "lon", None)),
        out_specs=P("lat", "lon", None, None),
        check_vma=False,
    )
```

time: 120 us -> 90.9 us (0.76)
  the two profiles are of different devices: /device:TPU:12 before, /device:TPU:28 now
where the time goes in v2:
time: 90.9 us; the launch traced here: 90.8 us
  Pallas kernels  86.3 us (95%)
  local copies, waits for them, and re-layouts  4.49 us (5%)
    pallas_call x1, Pallas kernels, on_device(): pl.pallas_call(functools.partial(layer_kernel, comm, compute), out_shape=...  86.3 us
    unnamed x1, local copies, waits for them, and re-layouts  1.87 us

profile of v2, /device:TPU:28, one launch (start us, length us, event | category | flops | bytes accessed | tf_op | source)
XLA Modules:
  0.0 90.8 jit_solution(14369337808646489461)
XLA Ops:
  0.0 1.4 %reshape.13.ids_hbm = s32[1,16]{1,0:T(1,128)} reshape(s32[1,2,8]{2,1,0:T(2,128)} %param.7) | data formatting | bytes 128 | tf_op jit(solution)/shard_map/reshape | solution.py:511
  1.4 1.3 %reshape.12.ids = s32[16]{0:T(128)} reshape(s32[1,2,8]{2,1,0:T(2,128)} %param.7) | data formatting | bytes 128 | tf_op jit(solution)/shard_map/reshape | solution.py:511
  2.6 86.3 %layer.1 = bf16[256,1024]{1,0:T(8,128)(2,1)} custom-call(s32[16]{0:T(128)} %reshape.12.ids, s32[1,16]{1,0:T(1,128)} %reshape.13.ids_hbm, bf16[2,128,1024]{2,1,0:T(8,128)(2,1)} %bitcast.3, bf16[1024,3072]{1,0:T(8,128)(2,1)} %wqkv.1, bf16[1024,1024]{1,0:T(8,128)(2,1)} %wout.1), custom_call_target="tpu_custom_call" | custom-call | tf_op jit(solution)/shard_map/layer/pallas_call | solution.py:470
  88.9 1.9 %copy.6 = bf16[1,2,128,1024]{3,2,1,0:T(8,128)(2,1)} copy(bf16[1,2,128,1024]{3,2,1,0:T(8,128)(2,1)} %bitcast.2) | data formatting | bytes 1048576

commit v3 on v2

--- a/solution.py
+++ b/solution.py
@@ -34,7 +34,6 @@
     ids_hbm,
     tok,
     wqkv,
-    wout,
     out,
     g,
     nb,
@@ -42,7 +41,6 @@
     picked,
     wq,
     wvt,
-    wo,
     x,
     kn,
     vn,
@@ -52,7 +50,6 @@
     ms,
     ls,
     acc,
-    att,
     sb0,
     sb1,
     pk0,
@@ -69,7 +66,7 @@
 ):
     n_lat, n_lon = lax.axis_size("lat"), lax.axis_size("lon")
     n_z = n_lon // 2
-    width = wo.shape[0]
+    width = wq.shape[0]
     lat, lon = lax.axis_index("lat"), lax.axis_index("lon")
     z, y_hi = lon // 2, lon % 2
     core = lat % 2
@@ -88,7 +85,6 @@
     loads = [
         pltpu.make_async_copy(tok, g.at[lon], load_sem.at[0]),
         pltpu.make_async_copy(wqkv, wq, load_sem.at[1]),
-        pltpu.make_async_copy(wout, wo, load_sem.at[2]),
     ]
     for load in loads:
         load.start()
@@ -157,11 +153,11 @@
     send(tok.at[1], nb.at[2], n_sem.at[1], (lat_off, lon_right))
     send(tok.at[0], nb.at[3], n_sem.at[2], (lat_off, lon_left))
 
-    def lookup(owner, table=None):
+    def lookup(owner, table):
         col = jnp.int32(0)
         which = jnp.int32(0)
         for entry in range(2 * TELE):
-            value = ids[entry] if table is None else table[0, entry]
+            value = table[0, entry // TELE, entry % TELE]
             hit = lax.shift_right_logical(value, 1) == owner
             col = jnp.where(hit, value & 1, col)
             which = jnp.where(hit, jnp.int32(entry // TELE), which)
@@ -239,14 +235,14 @@
     def far(tiles, own=False):
         whiches = []
         for i, (owner, both, one) in enumerate(tiles):
-            col, which = lookup(owner)
+            col, which = lookup(owner, ids)
             whiches.append(which)
             rows = slice(i * BLOCK, (i + 1) * BLOCK)
             x[rows] = one[...] if both is None else jnp.where(col == 1, both[1], both[0])
         rows = pl.ds(0, len(tiles) * BLOCK)
         project(x.at[rows], kt.at[rows], vt.at[:, rows])
         if own:
-            col, which = lookup(lon)
+            col, which = lookup(lon, ids)
             last = slice(len(tiles) * BLOCK, (len(tiles) + 1) * BLOCK)
             whiches.append(which)
             kt[last] = jnp.where(col == 1, kn[0, BLOCK : 2 * BLOCK], kn[0, :BLOCK])
@@ -325,12 +321,7 @@
                 total = ls[j, pair]
                 even = acc[j, pair, 0] / total[:, :BLOCK]
                 odd = acc[j, pair, 1] / total[:, BLOCK:]
-                att[j * BLOCK : (j + 1) * BLOCK, cols] = jnp.concatenate([even, odd], axis=0).T.astype(BF)
-
-        @pl.loop(0, width // 256)
-        def _(step):
-            cols = pl.ds(pl.multiple_of(step * 256, 256), 256)
-            out[:, cols] = nn_dot(att[...], wo[:, cols]).astype(BF)
+                out[j * BLOCK : (j + 1) * BLOCK, cols] = jnp.concatenate([even, odd], axis=0).T.astype(BF)
 
     def onward(owner, col, direction):
         send_g(owner, col, up if direction > 0 else down)
@@ -364,43 +355,36 @@
     if compute:
         own_projection()
 
-    relay(1, 1)
     chip = (lat_chip, lon)
     send(kn.at[0, pl.ds(0, 256)], kn.at[1, pl.ds(0, 256)], chip_sem.at[0], chip)
     send(vn.at[0, :, pl.ds(0, 256)], vn.at[1, :, pl.ds(0, 256)], chip_sem.at[1], chip)
+    relay(1, 1)
     if comm:
         arrived(ids_in, ids_sem.at[0])
         table = pltpu.make_async_copy(ids_in, ids_across, ids_sem.at[1])
         table.start()
         table.wait()
-    relay(1, 0)
     arrived(kn.at[1, pl.ds(0, 256)], chip_sem.at[0])
     arrived(vn.at[1, :, pl.ds(0, 256)], chip_sem.at[1])
     if compute:
         near(lambda j: ((0, 0, 256), (1, 0, 256)), True)
+    relay(1, 0)
 
     wait_g(partner, 0)
     wait_g(partner, 1)
+    if compute:
+        far([both(0, 1), both(-1, 0), both(1, 0)], own=True)
+
+    relay(2, 1)
+    relay(2, 0)
     turn = 1 - 2 * y_hi
     ahead = (lat, lax.rem(z + turn + n_z, n_z) * 2 + y_hi)
     behind = (lat, lax.rem(z - turn + n_z, n_z) * 2 + y_hi)
     send_g(partner, 1 - y_hi, ahead)
-    if compute:
-        far([both(0, 1), both(-1, 0), both(1, 0)], own=True)
-
-    relay(2, 1)
-    relay(2, 0)
     select(0, at(-2, 0))
     select(1, at(2, 0))
-    wait_g(lax.rem(z - turn + n_z, n_z) * 2 + 1 - y_hi, 1 - y_hi)
-    if compute:
-        x[0:128] = g[lon_left, 1]
-        x[128:256] = g[lon_right, 0]
-        project(x.at[pl.ds(0, 256)], kn.at[0, pl.ds(256, 256)], vn.at[0, :, pl.ds(256, 256)])
     hand(0)
     hand(1)
-    send(kn.at[0, pl.ds(256, 256)], kn.at[1, pl.ds(256, 256)], chip_sem.at[2], chip)
-    send(vn.at[0, :, pl.ds(256, 256)], vn.at[1, :, pl.ds(256, 256)], chip_sem.at[3], chip)
 
     arrived(nb.at[pl.ds(0, 2)], n_sem.at[0])
     arrived(nb.at[2], n_sem.at[1])
@@ -411,13 +395,15 @@
             project(nb.reshape(4 * BLOCK, width), kn.at[2], vn.at[2])
             near(lambda j: ((2, 0, 256), (2, 256 + j * BLOCK, BLOCK)), False)
 
+    last = lax.rem(z + n_z - 3 * sign, n_z) * 2 + y_hi
+    beyond = (lat, lax.rem(z + n_z + sign, n_z) * 2 + y_hi)
     wait_g(at(-3, 0), 1)
     wait_g(at(3, 0), 1)
+    send_g(last, 1, beyond)
+    if compute:
+        far([both(-2, 0), both(2, 0)])
     wait_g(at(-3, 0), 0)
     wait_g(at(3, 0), 0)
-    last = lax.rem(z + n_z - 3 * sign, n_z) * 2 + y_hi
-    beyond = (lat, lax.rem(z + n_z + sign, n_z) * 2 + y_hi)
-    send_g(last, 1, beyond)
     send_g(last, 0, beyond)
     select(2, at(-3, 0))
     select(3, at(3, 0))
@@ -426,31 +412,39 @@
     send_g(partner, y_hi, behind)
     hand(2)
     hand(3)
-
-    arrived(kn.at[1, pl.ds(256, 256)], chip_sem.at[2])
-    arrived(vn.at[1, :, pl.ds(256, 256)], chip_sem.at[3])
-    if compute:
-        near(lambda j: ((0, 256 + j * BLOCK, BLOCK), (1, 256 + j * BLOCK, BLOCK)), False)
-
-    given(0)
-    given(1)
-    if compute:
-        far([both(-2, 0), both(2, 0), single(-2, 0), single(2, 1)])
-
+    if compute:
+        far([both(-3, 0), both(3, 0)])
+
+    wait_g(lax.rem(z - turn + n_z, n_z) * 2 + 1 - y_hi, 1 - y_hi)
+    if compute:
+        x[0:128] = g[lon_left, 1]
+        x[128:256] = g[lon_right, 0]
+        project(x.at[pl.ds(0, 256)], kn.at[0, pl.ds(256, 256)], vn.at[0, :, pl.ds(256, 256)])
     wait_g(at(4, 0), 1)
     wait_g(at(4, 0), 0)
     select(4, at(4, 0))
+    send(kn.at[0, pl.ds(256, 256)], kn.at[1, pl.ds(256, 256)], chip_sem.at[2], chip)
+    send(vn.at[0, :, pl.ds(256, 256)], vn.at[1, :, pl.ds(256, 256)], chip_sem.at[3], chip)
     hand(4)
-    if compute:
-        far([both(-3, 0), both(3, 0), both(4, 0)])
-
-    given(2)
-    given(3)
+
+    given(0)
+    given(1)
+    if compute:
+        far([single(-2, 0), single(2, 1), both(4, 0)])
+    arrived(kn.at[1, pl.ds(256, 256)], chip_sem.at[2])
+    arrived(vn.at[1, :, pl.ds(256, 256)], chip_sem.at[3])
+    if compute:
+        near(lambda j: ((0, 256 + j * BLOCK, BLOCK), (1, 256 + j * BLOCK, BLOCK)), False)
+
     wait_g(lax.rem(z + turn + n_z, n_z) * 2 + 1 - y_hi, 1 - y_hi)
     wait_g(at(-1, 1), y_hi)
     wait_g(at(1, 1), y_hi)
     if compute:
-        far([both(-1, 1), both(1, 1), single(-3, 2), single(3, 3)])
+        far([both(-1, 1), both(1, 1)])
+    given(2)
+    given(3)
+    if compute:
+        far([single(-3, 2), single(3, 3)])
     given(4)
     if compute:
         far([single(4, 4)])
@@ -467,10 +461,10 @@
     tokens = tokens.reshape(2, BLOCK, width)
     n_lon = lax.axis_size("lon")
     anywhere = pl.BlockSpec(memory_space=pl.ANY)
-    mixed = pl.pallas_call(
+    attended = pl.pallas_call(
         functools.partial(layer_kernel, comm, compute),
         out_shape=jax.ShapeDtypeStruct((2 * BLOCK, width), BF),
-        in_specs=[pl.BlockSpec(memory_space=pltpu.SMEM)] + [anywhere] * 4,
+        in_specs=[pl.BlockSpec(memory_space=pltpu.SMEM)] + [anywhere] * 3,
         out_specs=pl.BlockSpec(memory_space=pltpu.VMEM),
         scratch_shapes=[
             pltpu.VMEM((n_lon, 2, BLOCK, width), BF),
@@ -478,7 +472,6 @@
             pltpu.VMEM((5, BLOCK, width), BF),
             pltpu.VMEM((5, BLOCK, width), BF),
             pltpu.VMEM((width, 3 * width), BF),
-            pltpu.VMEM((width, width), BF),
             pltpu.VMEM((width, width), BF),
             pltpu.VMEM((4 * BLOCK, width), BF),
             pltpu.VMEM((3, 4 * BLOCK, width), BF),
@@ -489,26 +482,26 @@
             pltpu.VMEM((2, PAIRS, 1, 2 * BLOCK), F32),
             pltpu.VMEM((2, PAIRS, 1, 2 * BLOCK), F32),
             pltpu.VMEM((2, PAIRS, 2, HD, BLOCK), F32),
-            pltpu.VMEM((2 * BLOCK, width), BF),
             pltpu.VMEM((8 * BLOCK, 2 * BLOCK), F32),
             pltpu.VMEM((8 * BLOCK, 2 * BLOCK), F32),
             pltpu.VMEM((4, 1, 2 * BLOCK), F32),
             pltpu.VMEM((4, 1, 2 * BLOCK), F32),
-            pltpu.VMEM((1, 2 * TELE), jnp.int32),
-            pltpu.SMEM((1, 2 * TELE), jnp.int32),
+            pltpu.VMEM((1, 2, TELE), jnp.int32),
+            pltpu.SMEM((1, 2, TELE), jnp.int32),
             pltpu.SemaphoreType.DMA((SENDS,)),
             pltpu.SemaphoreType.DMA((n_lon, 2)),
             pltpu.SemaphoreType.DMA((3,)),
             pltpu.SemaphoreType.DMA((4,)),
             pltpu.SemaphoreType.DMA((5,)),
             pltpu.SemaphoreType.DMA((2,)),
-            pltpu.SemaphoreType.DMA((3,)),
+            pltpu.SemaphoreType.DMA((2,)),
         ],
         compiler_params=pltpu.CompilerParams(
             collective_id=0 if comm else None, has_side_effects=True, vmem_limit_bytes=60 * 1024 * 1024
         ),
         name="layer",
-    )(tele_ids.reshape(-1), tele_ids.reshape(1, -1), tokens, w_qkv, w_out)
+    )(tele_ids, tele_ids, tokens, w_qkv)
+    mixed = jnp.dot(attended, w_out, preferred_element_type=F32).astype(BF)
     return mixed.reshape(shape)
 
 

time: 90.9 us -> 90.3 us (level)
  the two profiles are of different devices: /device:TPU:28 before, /device:TPU:10 now
where the time goes in v3:
time: 90.3 us; the launch traced here: 90.2 us
  Pallas kernels  87.6 us (97%)
  matrix products  2.55 us (3%)
    pallas_call x1, Pallas kernels, on_device(): pl.pallas_call(functools.partial(layer_kernel, comm, compute), out_shape=...  87.6 us
    dot_general x1, matrix products, on_device(): mixed = jnp.dot(attended, w_out, preferred_element_type=F32).astype(BF)  2.55 us

profile of v3, /device:TPU:10, one launch (start us, length us, event | category | flops | bytes accessed | tf_op | source)
XLA Modules:
  0.0 90.2 jit_solution(2337463250986641496)
XLA Ops:
  0.0 0.0 copy-start
  0.0 87.6 %layer.1 = bf16[256,1024]{1,0:T(8,128)(2,1)} custom-call(s32[1,2,8]{2,1,0:T(2,128)} %ids_hbm.1, s32[1,2,8]{2,1,0:T(2,128)} %ids_hbm.1, bf16[2,128,1024]{2,1,0:T(8,128)(2,1)} %bitcast.4, bf16[1024,3072]{1,0:T(8,128)(2,1)} %wqkv.1), custom_call_target="tpu_custom_call" | custom-call | tf_op jit(solution)/shard_map/layer/pallas_call | solution.py:464
  87.6 0.0 copy-done
  87.6 2.5 %convolution_convert_fusion = bf16[256,1024]{1,0:T(8,128)(2,1)} fusion(bf16[256,1024]{1,0:T(8,128)(2,1)} %layer.1, bf16[1024,1024]{1,0:T(8,128)(2,1)S(1)} %copy-done), kind=kOutput, calls=%fused_computation | convolution fusion | flops 537133056 | bytes 3145728 | tf_op jit(solution)/shard_map/dot_general | solution.py:504
Async XLA Ops:
  0.0 87.6 %copy-start = (bf16[1024,1024]{1,0:T(8,128)(2,1)S(1)}, bf16[1024,1024]{1,0:T(8,128)(2,1)}, u32[]{:S(2)}) copy-start(bf16[1024,1024]{1,0:T(8,128)(2,1)} %param.6) | copy-start | bytes 6291460

commit v4 on v3

--- a/solution.py
+++ b/solution.py
@@ -17,6 +17,7 @@
 SENDS = 40
 TELE = 8
 UNROLL = 2
+SPAN = 4
 
 
 def nt_dot(a, b):
@@ -143,15 +144,15 @@
         send(tok.at[col], g.at[lon, col], g_sem.at[lon, col], dev)
 
     send(ids_hbm, ids_in, ids_sem.at[0], across)
-    send_own(0, across)
-    send_own(1, across)
+    send(tok, nb.at[pl.ds(0, 2)], n_sem.at[0], (lat_off, lon))
+    send(tok.at[1], nb.at[2], n_sem.at[1], (lat_off, lon_right))
+    send(tok.at[0], nb.at[3], n_sem.at[2], (lat_off, lon_left))
     send_own(1, up)
     send_own(1, down)
     send_own(0, up)
     send_own(0, down)
-    send(tok, nb.at[pl.ds(0, 2)], n_sem.at[0], (lat_off, lon))
-    send(tok.at[1], nb.at[2], n_sem.at[1], (lat_off, lon_right))
-    send(tok.at[0], nb.at[3], n_sem.at[2], (lat_off, lon_left))
+    send_own(0, across)
+    send_own(1, across)
 
     def lookup(owner, table):
         col = jnp.int32(0)
@@ -177,12 +178,12 @@
     def pipelined(score, finish_pair):
         score(0, 0)
 
-        @pl.loop(0, PAIRS // 2)
+        @pl.loop(0, PAIRS // SPAN)
         def _(step):
-            score(2 * step + 1, 1)
-            finish_pair(2 * step, 0)
-            score(jnp.minimum(2 * step + 2, PAIRS - 1), 0)
-            finish_pair(2 * step + 1, 1)
+            for k in range(SPAN):
+                pair = step * SPAN + k
+                score(jnp.minimum(pair + 1, PAIRS - 1), (k + 1) % 2)
+                finish_pair(pair, k % 2)
 
     def near(keys_of, first):
         sizes = [size for _, _, size in keys_of(0)]
@@ -370,38 +371,38 @@
         near(lambda j: ((0, 0, 256), (1, 0, 256)), True)
     relay(1, 0)
 
+    arrived(nb.at[pl.ds(0, 2)], n_sem.at[0])
+    arrived(nb.at[2], n_sem.at[1])
+    arrived(nb.at[3], n_sem.at[2])
+    if compute:
+        @pl.when(off_inside)
+        def _():
+            project(nb.reshape(4 * BLOCK, width), kn.at[2], vn.at[2])
+            near(lambda j: ((2, 0, 256), (2, 256 + j * BLOCK, BLOCK)), False)
+
+    relay(2, 1)
+    relay(2, 0)
+    select(0, at(-2, 0))
+    select(1, at(2, 0))
+    hand(0)
+    hand(1)
+    if compute:
+        far([both(-1, 0), both(1, 0)], own=True)
+
     wait_g(partner, 0)
     wait_g(partner, 1)
-    if compute:
-        far([both(0, 1), both(-1, 0), both(1, 0)], own=True)
-
-    relay(2, 1)
-    relay(2, 0)
     turn = 1 - 2 * y_hi
     ahead = (lat, lax.rem(z + turn + n_z, n_z) * 2 + y_hi)
     behind = (lat, lax.rem(z - turn + n_z, n_z) * 2 + y_hi)
     send_g(partner, 1 - y_hi, ahead)
-    select(0, at(-2, 0))
-    select(1, at(2, 0))
-    hand(0)
-    hand(1)
-
-    arrived(nb.at[pl.ds(0, 2)], n_sem.at[0])
-    arrived(nb.at[2], n_sem.at[1])
-    arrived(nb.at[3], n_sem.at[2])
-    if compute:
-        @pl.when(off_inside)
-        def _():
-            project(nb.reshape(4 * BLOCK, width), kn.at[2], vn.at[2])
-            near(lambda j: ((2, 0, 256), (2, 256 + j * BLOCK, BLOCK)), False)
+    if compute:
+        far([both(0, 1), both(-2, 0), both(2, 0)])
 
     last = lax.rem(z + n_z - 3 * sign, n_z) * 2 + y_hi
     beyond = (lat, lax.rem(z + n_z + sign, n_z) * 2 + y_hi)
     wait_g(at(-3, 0), 1)
     wait_g(at(3, 0), 1)
     send_g(last, 1, beyond)
-    if compute:
-        far([both(-2, 0), both(2, 0)])
     wait_g(at(-3, 0), 0)
     wait_g(at(3, 0), 0)
     send_g(last, 0, beyond)
@@ -412,42 +413,36 @@
     send_g(partner, y_hi, behind)
     hand(2)
     hand(3)
-    if compute:
-        far([both(-3, 0), both(3, 0)])
-
+
+    given(0)
+    given(1)
+    if compute:
+        far([both(-3, 0), both(3, 0), single(-2, 0), single(2, 1)])
+    wait_g(at(4, 0), 1)
+    wait_g(at(4, 0), 0)
+    select(4, at(4, 0))
     wait_g(lax.rem(z - turn + n_z, n_z) * 2 + 1 - y_hi, 1 - y_hi)
+    hand(4)
     if compute:
         x[0:128] = g[lon_left, 1]
         x[128:256] = g[lon_right, 0]
         project(x.at[pl.ds(0, 256)], kn.at[0, pl.ds(256, 256)], vn.at[0, :, pl.ds(256, 256)])
-    wait_g(at(4, 0), 1)
-    wait_g(at(4, 0), 0)
-    select(4, at(4, 0))
+    wait_g(lax.rem(z + turn + n_z, n_z) * 2 + 1 - y_hi, 1 - y_hi)
     send(kn.at[0, pl.ds(256, 256)], kn.at[1, pl.ds(256, 256)], chip_sem.at[2], chip)
     send(vn.at[0, :, pl.ds(256, 256)], vn.at[1, :, pl.ds(256, 256)], chip_sem.at[3], chip)
-    hand(4)
-
-    given(0)
-    given(1)
-    if compute:
-        far([single(-2, 0), single(2, 1), both(4, 0)])
+    wait_g(at(-1, 1), y_hi)
+    wait_g(at(1, 1), y_hi)
+    if compute:
+        far([both(-1, 1), both(1, 1), both(4, 0)])
     arrived(kn.at[1, pl.ds(256, 256)], chip_sem.at[2])
     arrived(vn.at[1, :, pl.ds(256, 256)], chip_sem.at[3])
     if compute:
         near(lambda j: ((0, 256 + j * BLOCK, BLOCK), (1, 256 + j * BLOCK, BLOCK)), False)
-
-    wait_g(lax.rem(z + turn + n_z, n_z) * 2 + 1 - y_hi, 1 - y_hi)
-    wait_g(at(-1, 1), y_hi)
-    wait_g(at(1, 1), y_hi)
-    if compute:
-        far([both(-1, 1), both(1, 1)])
     given(2)
     given(3)
-    if compute:
-        far([single(-3, 2), single(3, 3)])
     given(4)
     if compute:
-        far([single(4, 4)])
+        far([single(-3, 2), single(3, 3), single(4, 4)])
         finish()
     else:
         out[...] = g[lon].reshape(out.shape)

time: 90.3 us -> 83.1 us (0.920)
  the two profiles are of different devices: /device:TPU:10 before, /device:TPU:1 now
where the time goes in v4:
time: 83.1 us; the launch traced here: 83 us
  Pallas kernels  80.4 us (97%)
  matrix products  2.55 us (3%)
    pallas_call x1, Pallas kernels, on_device(): pl.pallas_call(functools.partial(layer_kernel, comm, compute), out_shape=...  80.4 us
    dot_general x1, matrix products, on_device(): mixed = jnp.dot(attended, w_out, preferred_element_type=F32).astype(BF)  2.55 us

profile of v4, /device:TPU:1, one launch (start us, length us, event | category | flops | bytes accessed | tf_op | source)
XLA Modules:
  0.0 83.0 jit_solution(16136442086551333621)
XLA Ops:
  0.0 0.0 copy-start
  0.0 80.4 %layer.1 = bf16[256,1024]{1,0:T(8,128)(2,1)} custom-call(s32[1,2,8]{2,1,0:T(2,128)} %ids_hbm.1, s32[1,2,8]{2,1,0:T(2,128)} %ids_hbm.1, bf16[2,128,1024]{2,1,0:T(8,128)(2,1)} %bitcast.4, bf16[1024,3072]{1,0:T(8,128)(2,1)} %wqkv.1), custom_call_target="tpu_custom_call" | custom-call | tf_op jit(solution)/shard_map/layer/pallas_call | solution.py:459
  80.4 0.0 copy-done
  80.4 2.5 %convolution_convert_fusion = bf16[256,1024]{1,0:T(8,128)(2,1)} fusion(bf16[256,1024]{1,0:T(8,128)(2,1)} %layer.1, bf16[1024,1024]{1,0:T(8,128)(2,1)S(1)} %copy-done), kind=kOutput, calls=%fused_computation | convolution fusion | flops 537133056 | bytes 3145728 | tf_op jit(solution)/shard_map/dot_general | solution.py:499
Async XLA Ops:
  0.0 80.4 %copy-start = (bf16[1024,1024]{1,0:T(8,128)(2,1)S(1)}, bf16[1024,1024]{1,0:T(8,128)(2,1)}, u32[]{:S(2)}) copy-start(bf16[1024,1024]{1,0:T(8,128)(2,1)} %param.6) | copy-start | bytes 6291460

commit v5 on v4

--- a/solution.py
+++ b/solution.py
@@ -56,7 +56,7 @@
     pk0,
     pk1,
     ids_in,
-    ids_across,
+    ids_peers,
     send_sem,
     g_sem,
     n_sem,
@@ -143,7 +143,9 @@
     def send_own(col, dev):
         send(tok.at[col], g.at[lon, col], g_sem.at[lon, col], dev)
 
-    send(ids_hbm, ids_in, ids_sem.at[0], across)
+    send(ids_hbm, ids_in.at[0], ids_sem.at[0], across)
+    send(ids_hbm, ids_in.at[2], ids_sem.at[2], up)
+    send(ids_hbm, ids_in.at[1], ids_sem.at[1], down)
     send(tok, nb.at[pl.ds(0, 2)], n_sem.at[0], (lat_off, lon))
     send(tok.at[1], nb.at[2], n_sem.at[1], (lat_off, lon_right))
     send(tok.at[0], nb.at[3], n_sem.at[2], (lat_off, lon_left))
@@ -154,11 +156,11 @@
     send_own(0, across)
     send_own(1, across)
 
-    def lookup(owner, table):
+    def lookup(owner, table, peer=None):
         col = jnp.int32(0)
         which = jnp.int32(0)
         for entry in range(2 * TELE):
-            value = table[0, entry // TELE, entry % TELE]
+            value = table[0, entry // TELE, entry % TELE] if peer is None else table[peer, 0, entry // TELE, entry % TELE]
             hit = lax.shift_right_logical(value, 1) == owner
             col = jnp.where(hit, value & 1, col)
             which = jnp.where(hit, jnp.int32(entry // TELE), which)
@@ -333,13 +335,13 @@
         onward(at(-step, 0), col, 1)
         onward(at(step, 0), col, -1)
 
-    def select(slot, owner):
+    def select(slot, owner, peer):
         if comm:
-            col, _ = lookup(owner, ids_across)
+            col, _ = lookup(owner, ids_peers, peer)
             pick[slot] = jnp.where(col == 1, g[owner, 1], g[owner, 0])
 
-    def hand(slot):
-        send(pick.at[slot], picked.at[slot], pick_sem.at[slot], across)
+    def hand(slot, dev):
+        send(pick.at[slot], picked.at[slot], pick_sem.at[slot], dev)
 
     def given(slot):
         arrived(picked.at[slot], pick_sem.at[slot])
@@ -361,8 +363,9 @@
     send(vn.at[0, :, pl.ds(0, 256)], vn.at[1, :, pl.ds(0, 256)], chip_sem.at[1], chip)
     relay(1, 1)
     if comm:
-        arrived(ids_in, ids_sem.at[0])
-        table = pltpu.make_async_copy(ids_in, ids_across, ids_sem.at[1])
+        for peer in range(3):
+            arrived(ids_in.at[peer], ids_sem.at[peer])
+        table = pltpu.make_async_copy(ids_in, ids_peers, ids_sem.at[3])
         table.start()
         table.wait()
     arrived(kn.at[1, pl.ds(0, 256)], chip_sem.at[0])
@@ -382,10 +385,10 @@
 
     relay(2, 1)
     relay(2, 0)
-    select(0, at(-2, 0))
-    select(1, at(2, 0))
-    hand(0)
-    hand(1)
+    select(0, at(-2, 0), 0)
+    select(1, at(2, 0), 0)
+    hand(0, across)
+    hand(1, across)
     if compute:
         far([both(-1, 0), both(1, 0)], own=True)
 
@@ -393,7 +396,6 @@
     wait_g(partner, 1)
     turn = 1 - 2 * y_hi
     ahead = (lat, lax.rem(z + turn + n_z, n_z) * 2 + y_hi)
-    behind = (lat, lax.rem(z - turn + n_z, n_z) * 2 + y_hi)
     send_g(partner, 1 - y_hi, ahead)
     if compute:
         far([both(0, 1), both(-2, 0), both(2, 0)])
@@ -406,43 +408,45 @@
     wait_g(at(-3, 0), 0)
     wait_g(at(3, 0), 0)
     send_g(last, 0, beyond)
-    select(2, at(-3, 0))
-    select(3, at(3, 0))
-    send_g(partner, 1 - y_hi, behind)
-    send_g(partner, y_hi, ahead)
-    send_g(partner, y_hi, behind)
-    hand(2)
-    hand(3)
+    select(2, at(-3, 0), 0)
+    select(3, at(3, 0), 0)
+    select(5, partner, 1)
+    select(6, partner, 2)
+    hand(2, across)
+    hand(3, across)
+    hand(5, up)
+    hand(6, down)
 
     given(0)
     given(1)
     if compute:
         far([both(-3, 0), both(3, 0), single(-2, 0), single(2, 1)])
-    wait_g(at(4, 0), 1)
-    wait_g(at(4, 0), 0)
-    select(4, at(4, 0))
     wait_g(lax.rem(z - turn + n_z, n_z) * 2 + 1 - y_hi, 1 - y_hi)
-    hand(4)
     if compute:
         x[0:128] = g[lon_left, 1]
         x[128:256] = g[lon_right, 0]
         project(x.at[pl.ds(0, 256)], kn.at[0, pl.ds(256, 256)], vn.at[0, :, pl.ds(256, 256)])
-    wait_g(lax.rem(z + turn + n_z, n_z) * 2 + 1 - y_hi, 1 - y_hi)
+    wait_g(at(4, 0), 1)
+    wait_g(at(4, 0), 0)
+    select(4, at(4, 0), 0)
     send(kn.at[0, pl.ds(256, 256)], kn.at[1, pl.ds(256, 256)], chip_sem.at[2], chip)
     send(vn.at[0, :, pl.ds(256, 256)], vn.at[1, :, pl.ds(256, 256)], chip_sem.at[3], chip)
-    wait_g(at(-1, 1), y_hi)
-    wait_g(at(1, 1), y_hi)
-    if compute:
-        far([both(-1, 1), both(1, 1), both(4, 0)])
+    hand(4, across)
+    if compute:
+        far([both(4, 0)])
     arrived(kn.at[1, pl.ds(256, 256)], chip_sem.at[2])
     arrived(vn.at[1, :, pl.ds(256, 256)], chip_sem.at[3])
     if compute:
         near(lambda j: ((0, 256 + j * BLOCK, BLOCK), (1, 256 + j * BLOCK, BLOCK)), False)
+    given(5)
+    given(6)
     given(2)
     given(3)
+    if compute:
+        far([single(-1, 5), single(1, 6), single(-3, 2), single(3, 3)])
     given(4)
     if compute:
-        far([single(-3, 2), single(3, 3), single(4, 4)])
+        far([single(4, 4)])
         finish()
     else:
         out[...] = g[lon].reshape(out.shape)
@@ -464,8 +468,8 @@
         scratch_shapes=[
             pltpu.VMEM((n_lon, 2, BLOCK, width), BF),
             pltpu.VMEM((4, BLOCK, width), BF),
-            pltpu.VMEM((5, BLOCK, width), BF),
-            pltpu.VMEM((5, BLOCK, width), BF),
+            pltpu.VMEM((7, BLOCK, width), BF),
+            pltpu.VMEM((7, BLOCK, width), BF),
             pltpu.VMEM((width, 3 * width), BF),
             pltpu.VMEM((width, width), BF),
             pltpu.VMEM((4 * BLOCK, width), BF),
@@ -481,14 +485,14 @@
             pltpu.VMEM((8 * BLOCK, 2 * BLOCK), F32),
             pltpu.VMEM((4, 1, 2 * BLOCK), F32),
             pltpu.VMEM((4, 1, 2 * BLOCK), F32),
-            pltpu.VMEM((1, 2, TELE), jnp.int32),
-            pltpu.SMEM((1, 2, TELE), jnp.int32),
+            pltpu.VMEM((3, 1, 2, TELE), jnp.int32),
+            pltpu.SMEM((3, 1, 2, TELE), jnp.int32),
             pltpu.SemaphoreType.DMA((SENDS,)),
             pltpu.SemaphoreType.DMA((n_lon, 2)),
             pltpu.SemaphoreType.DMA((3,)),
             pltpu.SemaphoreType.DMA((4,)),
-            pltpu.SemaphoreType.DMA((5,)),
-            pltpu.SemaphoreType.DMA((2,)),
+            pltpu.SemaphoreType.DMA((7,)),
+            pltpu.SemaphoreType.DMA((4,)),
             pltpu.SemaphoreType.DMA((2,)),
         ],
         compiler_params=pltpu.CompilerParams(

time: 83.1 us -> 81.5 us (0.981)
  Pallas kernels: 80.4 us -> 78.3 us
    pallas_call x1, Pallas kernels: 80.4 us -> 78.3 us  [on_device(): pl.pallas_call(functools.partial(layer_kernel, comm, compute), out_shape=...]
where the time goes in v5:
time: 81.5 us; the launch traced here: 80.9 us
  Pallas kernels  78.3 us (96%)
  matrix products  2.55 us (3%)
    pallas_call x1, Pallas kernels, on_device(): pl.pallas_call(functools.partial(layer_kernel, comm, compute), out_shape=...  78.3 us
    dot_general x1, matrix products, on_device(): mixed = jnp.dot(attended, w_out, preferred_element_type=F32).astype(BF)  2.55 us

profile of v5, /device:TPU:1, one launch (start us, length us, event | category | flops | bytes accessed | tf_op | source)
XLA Modules:
  0.0 80.9 jit_solution(13200145492893101547)
XLA Ops:
  0.0 0.0 copy-start
  0.0 78.3 %layer.1 = bf16[256,1024]{1,0:T(8,128)(2,1)} custom-call(s32[1,2,8]{2,1,0:T(2,128)} %ids_hbm.1, s32[1,2,8]{2,1,0:T(2,128)} %ids_hbm.1, bf16[2,128,1024]{2,1,0:T(8,128)(2,1)} %bitcast.4, bf16[1024,3072]{1,0:T(8,128)(2,1)} %wqkv.1), custom_call_target="tpu_custom_call" | custom-call | tf_op jit(solution)/shard_map/layer/pallas_call | solution.py:463
  78.3 0.0 copy-done
  78.4 2.5 %convolution_convert_fusion = bf16[256,1024]{1,0:T(8,128)(2,1)} fusion(bf16[256,1024]{1,0:T(8,128)(2,1)} %layer.1, bf16[1024,1024]{1,0:T(8,128)(2,1)S(1)} %copy-done), kind=kOutput, calls=%fused_computation | convolution fusion | flops 537133056 | bytes 3145728 | tf_op jit(solution)/shard_map/dot_general | solution.py:503
Async XLA Ops:
  0.0 78.3 %copy-start = (bf16[1024,1024]{1,0:T(8,128)(2,1)S(1)}, bf16[1024,1024]{1,0:T(8,128)(2,1)}, u32[]{:S(2)}) copy-start(bf16[1024,1024]{1,0:T(8,128)(2,1)} %param.6) | copy-start | bytes 6291460

commit v6 on v5

--- a/solution.py
+++ b/solution.py
@@ -398,7 +398,10 @@
     ahead = (lat, lax.rem(z + turn + n_z, n_z) * 2 + y_hi)
     send_g(partner, 1 - y_hi, ahead)
     if compute:
-        far([both(0, 1), both(-2, 0), both(2, 0)])
+        far([both(-2, 0), both(2, 0)])
+    given(0)
+    if compute:
+        far([both(0, 1), single(-2, 0)])
 
     last = lax.rem(z + n_z - 3 * sign, n_z) * 2 + y_hi
     beyond = (lat, lax.rem(z + n_z + sign, n_z) * 2 + y_hi)
@@ -417,33 +420,32 @@
     hand(5, up)
     hand(6, down)
 
-    given(0)
-    given(1)
-    if compute:
-        far([both(-3, 0), both(3, 0), single(-2, 0), single(2, 1)])
+    if compute:
+        far([both(-3, 0), both(3, 0)])
     wait_g(lax.rem(z - turn + n_z, n_z) * 2 + 1 - y_hi, 1 - y_hi)
     if compute:
         x[0:128] = g[lon_left, 1]
         x[128:256] = g[lon_right, 0]
         project(x.at[pl.ds(0, 256)], kn.at[0, pl.ds(256, 256)], vn.at[0, :, pl.ds(256, 256)])
+    given(1)
+    given(2)
+    send(kn.at[0, pl.ds(256, 256)], kn.at[1, pl.ds(256, 256)], chip_sem.at[2], chip)
+    send(vn.at[0, :, pl.ds(256, 256)], vn.at[1, :, pl.ds(256, 256)], chip_sem.at[3], chip)
+    if compute:
+        far([single(2, 1), single(-3, 2)])
     wait_g(at(4, 0), 1)
     wait_g(at(4, 0), 0)
     select(4, at(4, 0), 0)
-    send(kn.at[0, pl.ds(256, 256)], kn.at[1, pl.ds(256, 256)], chip_sem.at[2], chip)
-    send(vn.at[0, :, pl.ds(256, 256)], vn.at[1, :, pl.ds(256, 256)], chip_sem.at[3], chip)
-    hand(4, across)
-    if compute:
-        far([both(4, 0)])
     arrived(kn.at[1, pl.ds(256, 256)], chip_sem.at[2])
     arrived(vn.at[1, :, pl.ds(256, 256)], chip_sem.at[3])
+    hand(4, across)
     if compute:
         near(lambda j: ((0, 256 + j * BLOCK, BLOCK), (1, 256 + j * BLOCK, BLOCK)), False)
     given(5)
     given(6)
-    given(2)
     given(3)
     if compute:
-        far([single(-1, 5), single(1, 6), single(-3, 2), single(3, 3)])
+        far([both(4, 0), single(-1, 5), single(1, 6), single(3, 3)])
     given(4)
     if compute:
         far([single(4, 4)])
@@ -460,6 +462,7 @@
     tokens = tokens.reshape(2, BLOCK, width)
     n_lon = lax.axis_size("lon")
     anywhere = pl.BlockSpec(memory_space=pl.ANY)
+    hbm = pltpu.with_memory_space_constraint
     attended = pl.pallas_call(
         functools.partial(layer_kernel, comm, compute),
         out_shape=jax.ShapeDtypeStruct((2 * BLOCK, width), BF),
@@ -496,10 +499,10 @@
             pltpu.SemaphoreType.DMA((2,)),
         ],
         compiler_params=pltpu.CompilerParams(
-            collective_id=0 if comm else None, has_side_effects=True, vmem_limit_bytes=60 * 1024 * 1024
+            collective_id=0 if comm else None, has_side_effects=True, vmem_limit_bytes=44 * 1024 * 1024
         ),
         name="layer",
-    )(tele_ids, tele_ids, tokens, w_qkv)
+    )(tele_ids, hbm(tele_ids, pltpu.HBM), hbm(tokens, pltpu.HBM), hbm(w_qkv, pltpu.HBM))
     mixed = jnp.dot(attended, w_out, preferred_element_type=F32).astype(BF)
     return mixed.reshape(shape)
 

time: 81.5 us -> 77.6 us (0.952)
  Pallas kernels: 78.3 us -> 75.8 us
  matrix products: 2.55 us -> 1.51 us
    pallas_call x1, Pallas kernels: 78.3 us -> 75.8 us  [on_device(): pl.pallas_call(functools.partial(layer_kernel, comm, compute), out_shape=...]
    dot_general x1, matrix products: 2.55 us -> 1.51 us  [on_device(): mixed = jnp.dot(attended, w_out, preferred_element_type=F32).astype(BF)]
where the time goes in v6:
time: 77.6 us; the launch traced here: 77.3 us
  Pallas kernels  75.8 us (98%)
  matrix products  1.51 us (2%)
    pallas_call x1, Pallas kernels, on_device(): pl.pallas_call(functools.partial(layer_kernel, comm, compute), out_shape=...  75.8 us

profile of v6, /device:TPU:1, one launch (start us, length us, event | category | flops | bytes accessed | tf_op | source)
XLA Modules:
  0.0 77.3 jit_solution(12838155256685625940)
XLA Ops:
  0.0 0.0 copy-start
  0.0 75.8 %layer.1 = bf16[256,1024]{1,0:T(8,128)(2,1)S(1)} custom-call(s32[1,2,8]{2,1,0:T(2,128)} %ids_hbm.1, s32[1,2,8]{2,1,0:T(2,128)} %ids_hbm.1, bf16[2,128,1024]{2,1,0:T(8,128)(2,1)} %bitcast.4, bf16[1024,3072]{1,0:T(8,128)(2,1)} %wqkv.1), custom_call_target="tpu_custom_call" | custom-call | tf_op jit(solution)/shard_map/layer/pallas_call | solution.py:466
  75.8 0.0 copy-done
  75.8 1.5 %convolution_convert_fusion = bf16[256,1024]{1,0:T(8,128)(2,1)} fusion(bf16[256,1024]{1,0:T(8,128)(2,1)S(1)} %layer.1, bf16[1024,1024]{1,0:T(8,128)(2,1)S(1)} %copy-done), kind=kOutput, calls=%fused_computation | convolution fusion | flops 537133056 | bytes 3145728 | tf_op jit(solution)/shard_map/dot_general | solution.py:506
Async XLA Ops:
  0.0 75.8 %copy-start = (bf16[1024,1024]{1,0:T(8,128)(2,1)S(1)}, bf16[1024,1024]{1,0:T(8,128)(2,1)}, u32[]{:S(2)}) copy-start(bf16[1024,1024]{1,0:T(8,128)(2,1)} %param.6) | copy-start | bytes 6291460

commit v7 on v6

--- a/solution.py
+++ b/solution.py
@@ -187,6 +187,14 @@
                 score(jnp.minimum(pair + 1, PAIRS - 1), (k + 1) % 2)
                 finish_pair(pair, k % 2)
 
+    def together(score, finish_pair):
+        @pl.loop(0, PAIRS // SPAN)
+        def _(step):
+            for k in range(SPAN):
+                score(step * SPAN + k, k)
+            for k in range(SPAN):
+                finish_pair(step * SPAN + k, k)
+
     def near(keys_of, first):
         sizes = [size for _, _, size in keys_of(0)]
         count = sum(sizes)
@@ -212,17 +220,16 @@
                 if not first:
                     before = ms[j, pair]
                     peak = jnp.maximum(peak, before)
-                total = None
                 summed = None
                 offset = j * count
                 for row, start, size in keys_of(j):
                     expos = jnp.exp(sb[slot][pl.ds(offset, size)] - peak)
-                    part = jnp.sum(expos, axis=0, keepdims=True)
-                    prod = nn_dot(vn[row, cols, pl.ds(start, size)], expos.astype(BF))
-                    total = part if total is None else total + part
+                    values = jnp.concatenate([vn[row, cols, pl.ds(start, size)], jnp.ones((16, size), BF)], axis=0)
+                    prod = nn_dot(values, expos.astype(BF))
                     summed = prod if summed is None else summed + prod
                     offset += size
-                even, odd = summed[:HD, :BLOCK], summed[HD:, BLOCK:]
+                total = summed[BLOCK : BLOCK + 1]
+                even, odd = summed[:HD, :BLOCK], summed[HD:BLOCK, BLOCK:]
                 if not first:
                     decay = jnp.exp(before - peak)
                     total = total + ls[j, pair] * decay
@@ -253,16 +260,19 @@
         count = len(whiches)
         keys = count * BLOCK
 
+        def base(slot):
+            return slot // 2 * 4 * BLOCK
+
         def score(pair, slot):
             cols = pair_cols(pair)
             for i in range(count):
                 s = nn_dot(kt[i * BLOCK : (i + 1) * BLOCK, cols], qmt[whiches[i], pair])
-                sb[slot][i * BLOCK : (i + 1) * BLOCK] = s
-                pk[slot][i] = jnp.max(s, axis=0, keepdims=True)
+                sb[slot % 2][base(slot) + i * BLOCK : base(slot) + (i + 1) * BLOCK] = s
+                pk[slot % 2][slot // 2 * 2 + i] = jnp.max(s, axis=0, keepdims=True)
 
         def finish_pair(pair, slot):
             cols = pair_cols(pair)
-            peaks = [pk[slot][i] for i in range(count)]
+            peaks = [pk[slot % 2][slot // 2 * 2 + i] for i in range(count)]
             before = [ms[j, pair] for j in range(2)]
             now = []
             for j in range(2):
@@ -275,7 +285,7 @@
             weights = [[], []]
             for i in range(count):
                 mine = whiches[i] == 0
-                expos = jnp.exp(sb[slot][i * BLOCK : (i + 1) * BLOCK] - jnp.where(mine, now[0], now[1]))
+                expos = jnp.exp(sb[slot % 2][base(slot) + i * BLOCK : base(slot) + (i + 1) * BLOCK] - jnp.where(mine, now[0], now[1]))
                 part = jnp.sum(expos, axis=0, keepdims=True)
                 rounded = expos.astype(BF)
                 none = jnp.zeros_like(rounded)
@@ -290,7 +300,10 @@
                 acc[j, pair, 0] = acc[j, pair, 0] * decay[j][:, :BLOCK] + summed[:HD, :BLOCK]
                 acc[j, pair, 1] = acc[j, pair, 1] * decay[j][:, BLOCK:] + summed[HD:, BLOCK:]
 
-        pipelined(score, finish_pair)
+        if count <= 2:
+            together(score, finish_pair)
+        else:
+            pipelined(score, finish_pair)
 
     def own_projection():
         own = g.at[lon]
@@ -441,11 +454,13 @@
     hand(4, across)
     if compute:
         near(lambda j: ((0, 256 + j * BLOCK, BLOCK), (1, 256 + j * BLOCK, BLOCK)), False)
+    given(3)
+    if compute:
+        far([both(4, 0), single(3, 3)])
     given(5)
     given(6)
-    given(3)
-    if compute:
-        far([both(4, 0), single(-1, 5), single(1, 6), single(3, 3)])
+    if compute:
+        far([single(-1, 5), single(1, 6)])
     given(4)
     if compute:
         far([single(4, 4)])

time: 77.6 us -> 76.7 us (0.988)
  no operation moved by 1% of the time
where the time goes in v7:
time: 76.7 us; the launch traced here: 76.6 us
  Pallas kernels  75.1 us (98%)
  matrix products  1.51 us (2%)
    pallas_call x1, Pallas kernels, on_device(): pl.pallas_call(functools.partial(layer_kernel, comm, compute), out_shape=...  75.1 us

profile of v7, /device:TPU:1, one launch (start us, length us, event | category | flops | bytes accessed | tf_op | source)
XLA Modules:
  0.0 76.6 jit_solution(13550073607566875361)
XLA Ops:
  0.0 0.0 copy-start
  0.0 75.1 %layer.1 = bf16[256,1024]{1,0:T(8,128)(2,1)S(1)} custom-call(s32[1,2,8]{2,1,0:T(2,128)} %ids_hbm.1, s32[1,2,8]{2,1,0:T(2,128)} %ids_hbm.1, bf16[2,128,1024]{2,1,0:T(8,128)(2,1)} %bitcast.4, bf16[1024,3072]{1,0:T(8,128)(2,1)} %wqkv.1), custom_call_target="tpu_custom_call" | custom-call | tf_op jit(solution)/shard_map/layer/pallas_call | solution.py:481
  75.1 0.0 copy-done
  75.1 1.5 %convolution_convert_fusion = bf16[256,1024]{1,0:T(8,128)(2,1)} fusion(bf16[256,1024]{1,0:T(8,128)(2,1)S(1)} %layer.1, bf16[1024,1024]{1,0:T(8,128)(2,1)S(1)} %copy-done), kind=kOutput, calls=%fused_computation | convolution fusion | flops 537133056 | bytes 3145728 | tf_op jit(solution)/shard_map/dot_general | solution.py:521
Async XLA Ops:
  0.0 75.1 %copy-start = (bf16[1024,1024]{1,0:T(8,128)(2,1)S(1)}, bf16[1024,1024]{1,0:T(8,128)(2,1)}, u32[]{:S(2)}) copy-start(bf16[1024,1024]{1,0:T(8,128)(2,1)} %param.6) | copy-start | bytes 6291460
